TPU v7x, 256 devices: a whole 4x4x8 slice. The times are simulated.
256 devices in a mesh: gz: 8 (over x, core), gx: 32 (over z, y).
Axes of the slice: x: 4, y: 4, z: 8, core: 2. Of those that a mesh axis runs over, the one named last changes fastest.
Arguments:
- volume: float32 [256, 512, 256], P('gz', 'gx')
- measured: float32 [2, 256, 2048], P(None, 'gz')
- weight_blocks: bfloat16 [64, 128, 128], replicated, may hold values from 0 to 2
- view_order: int32 [2], replicated, may hold values from 0 to 1, each once
- tile_voxel: int32 [2, 8, 16384], P(None, 'gz', 'gx'), may hold values from 0 to 1023
- tile_column: int32 [2, 8, 16384], P(None, 'gz', 'gx'), may hold values from 0 to 15
- tile_block: int32 [2, 8, 16384], P(None, 'gz', 'gx'), may hold values from 0 to 63
- entry_count: int32 [2, 8, 32], P(None, 'gz', 'gx'), may hold values from 1 to 512, as said below
Outputs:
- volume_out: float32 [256, 512, 256], P('gz', 'gx')
Inputs may be any that keep to these rules, and one draw needn't show every extreme that they name: Entries of block (a, c) of view v at or past entry_count[v, a, c] are not used; in every view some block has 512 live entries.
All inputs are finite; a program needn't handle non-finite values.
Results may differ from a plain program's by a relative error of at most 0.0027.
Values may be sent and summed in bfloat16 or wider, within the bound.
A program may use at most 64 MiB of HBM per device.

v0:
```python
import functools

import jax
import jax.numpy as jnp
from jax import lax
from jax.experimental import pallas as pl
from jax.experimental.pallas import tpu as pltpu
from jax.sharding import PartitionSpec as P

TV_STEPS = 4


smooth_floor = 0.01
step_gain = 0.25
norm_floor = 1e-06
group_rows = 128


MESH = pl.DeviceIdType.MESH


def _peer(axis, position):
    if axis == "gz":
        return (position, lax.axis_index("gx"))
    return (lax.axis_index("gz"), position)


def vector_sum_kernel(n, x_ref, o_ref, recv, red, gath, ssem1, rsem1, ssem2, rsem2):
    me = lax.axis_index("gx")
    barrier = pltpu.get_barrier_semaphore()
    for d in range(1, n):
        pl.semaphore_signal(barrier, inc=1, device_id=_peer("gx", lax.rem(me + d, n)), device_id_type=MESH)
    pl.semaphore_wait(barrier, n - 1)
    sends = []
    for d in range(1, n):
        dst = lax.rem(me + d, n)
        copy = pltpu.make_async_remote_copy(
            src_ref=x_ref.at[dst], dst_ref=recv.at[d], send_sem=ssem1.at[d], recv_sem=rsem1.at[d],
            device_id=_peer("gx", dst), device_id_type=MESH)
        copy.start()
        sends.append(copy)
    for copy in sends:
        copy.wait()
    total = x_ref[me].astype(jnp.float32)
    for d in range(1, n):
        total = total + recv[d].astype(jnp.float32)
    red[...] = total.astype(red.dtype)
    sends = []
    for d in range(1, n):
        dst = lax.rem(me + d, n)
        copy = pltpu.make_async_remote_copy(
            src_ref=red, dst_ref=gath.at[me], send_sem=ssem2.at[d], recv_sem=rsem2.at[d],
            device_id=_peer("gx", dst), device_id_type=MESH)
        copy.start()
        sends.append(copy)
    for copy in sends:
        copy.wait()
    gath[me] = red[...]
    o_ref[...] = gath[...]


def vector_sum(x):
    n, rows, cols = x.shape
    return pl.pallas_call(
        functools.partial(vector_sum_kernel, n),
        out_shape=jax.ShapeDtypeStruct(x.shape, x.dtype),
        in_specs=[pl.BlockSpec(memory_space=pltpu.VMEM)],
        out_specs=pl.BlockSpec(memory_space=pltpu.VMEM),
        scratch_shapes=[
            pltpu.VMEM(x.shape, x.dtype),
            pltpu.VMEM((rows, cols), x.dtype),
            pltpu.VMEM(x.shape, x.dtype),
            pltpu.SemaphoreType.DMA((n,)),
            pltpu.SemaphoreType.DMA((n,)),
            pltpu.SemaphoreType.DMA((n,)),
            pltpu.SemaphoreType.DMA((n,)),
        ],
        compiler_params=pltpu.CompilerParams(collective_id=1, has_side_effects=True),
    )(x)


def _stage_peers(stage):
    axis, stride, size = stage
    index = lax.axis_index(axis)
    position = lax.rem(index // stride, size)
    base = index - position * stride
    return [base + lax.rem(position + d, size) * stride for d in range(1, size)]


def scalar_sum_kernel(stages, x_ref, o_ref, buf, recv, ssem, rsem):
    barrier = pltpu.get_barrier_semaphore()
    count = 0
    for stage in stages:
        for peer in _stage_peers(stage):
            pl.semaphore_signal(barrier, inc=1, device_id=_peer(stage[0], peer), device_id_type=MESH)
            count += 1
    pl.semaphore_wait(barrier, count)
    total = x_ref[...]
    slot = 0
    for s, stage in enumerate(stages):
        axis, stride, size = stage
        position = lax.rem(lax.axis_index(axis) // stride, size)
        source = x_ref if s == 0 else buf.at[s - 1]
        recv[slot] = total
        sends = []
        for d, peer in enumerate(_stage_peers(stage), start=1):
            copy = pltpu.make_async_remote_copy(
                src_ref=source, dst_ref=recv.at[slot + d], send_sem=ssem.at[slot + d],
                recv_sem=rsem.at[slot + d], device_id=_peer(axis, peer), device_id_type=MESH)
            copy.start()
            sends.append(copy)
        for copy in sends:
            copy.wait()
        total = recv[slot + position]
        for p in range(1, size):
            total = total + recv[slot + lax.rem(position - p + size, size)]
        slot += size
        if s + 1 < len(stages):
            buf[s] = total
    o_ref[...] = total


def scalar_sum(x, stages):
    slots = sum(size for _, _, size in stages)
    return pl.pallas_call(
        functools.partial(scalar_sum_kernel, stages),
        out_shape=jax.ShapeDtypeStruct(x.shape, x.dtype),
        in_specs=[pl.BlockSpec(memory_space=pltpu.VMEM)],
        out_specs=pl.BlockSpec(memory_space=pltpu.VMEM),
        scratch_shapes=[
            pltpu.VMEM((max(len(stages) - 1, 1),) + x.shape, x.dtype),
            pltpu.VMEM((slots,) + x.shape, x.dtype),
            pltpu.SemaphoreType.DMA((slots,)),
            pltpu.SemaphoreType.DMA((slots,)),
        ],
        cost_estimate=pl.CostEstimate(flops=0, transcendentals=0, bytes_accessed=40_000_000),
        compiler_params=pltpu.CompilerParams(collective_id=2, has_side_effects=True),
    )(x)


def halo_routes(depth, width):
    count_z, count_x = lax.axis_size("gz"), lax.axis_size("gx")
    z, x = lax.axis_index("gz"), lax.axis_index("gx")
    up_z, down_z = lax.rem(z + 1, count_z), lax.rem(z + count_z - 1, count_z)
    up_x, down_x = lax.rem(x + 1, count_x), lax.rem(x + count_x - 1, count_x)
    return [
        (0, depth, (up_z, x)),
        (depth, depth, (down_z, x)),
        (2 * depth, width, (z, up_x)),
        (2 * depth + width, width, (z, down_x)),
        (2 * depth + 2 * width, 1, (up_z, down_x)),
        (2 * depth + 2 * width + 1, 1, (down_z, up_x)),
    ]


def tv_exchange_kernel(stages, shape, x_ref, f_ref, o_ref, h_ref, buf, recv, ssem, rsem, hrecv, hsend, hget):
    routes = halo_routes(*shape)
    barrier = pltpu.get_barrier_semaphore()
    count = 0
    for stage in stages:
        for peer in _stage_peers(stage):
            pl.semaphore_signal(barrier, inc=1, device_id=_peer(stage[0], peer), device_id_type=MESH)
            count += 1
    for _, _, target in routes:
        pl.semaphore_signal(barrier, inc=1, device_id=target, device_id_type=MESH)
        count += 1
    pl.semaphore_wait(barrier, count)
    halo = []
    for k, (row, rows, target) in enumerate(routes):
        copy = pltpu.make_async_remote_copy(
            src_ref=f_ref.at[pl.ds(row, rows)], dst_ref=hrecv.at[pl.ds(row, rows)],
            send_sem=hsend.at[k], recv_sem=hget.at[k], device_id=target, device_id_type=MESH)
        copy.start()
        halo.append(copy)
    total = x_ref[...]
    slot = 0
    for s, stage in enumerate(stages):
        axis, stride, size = stage
        position = lax.rem(lax.axis_index(axis) // stride, size)
        source = x_ref if s == 0 else buf.at[s - 1]
        recv[slot] = total
        sends = []
        for d, peer in enumerate(_stage_peers(stage), start=1):
            copy = pltpu.make_async_remote_copy(
                src_ref=source, dst_ref=recv.at[slot + d], send_sem=ssem.at[slot + d],
                recv_sem=rsem.at[slot + d], device_id=_peer(axis, peer), device_id_type=MESH)
            copy.start()
            sends.append(copy)
        for copy in sends:
            copy.wait()
        total = recv[slot + position]
        for p in range(1, size):
            total = total + recv[slot + lax.rem(position - p + size, size)]
        slot += size
        if s + 1 < len(stages):
            buf[s] = total
    o_ref[...] = total
    for copy in halo:
        copy.wait()
    h_ref[...] = hrecv[...]


def tv_exchange(x, cells, stages):
    faces = faces_of(cells)
    slots = sum(size for _, _, size in stages)
    return pl.pallas_call(
        functools.partial(tv_exchange_kernel, stages, (cells.shape[1], cells.shape[0])),
        out_shape=(jax.ShapeDtypeStruct(x.shape, x.dtype), jax.ShapeDtypeStruct(faces.shape, faces.dtype)),
        in_specs=[pl.BlockSpec(memory_space=pltpu.VMEM)] * 2,
        out_specs=(pl.BlockSpec(memory_space=pltpu.VMEM), pl.BlockSpec(memory_space=pltpu.VMEM)),
        scratch_shapes=[
            pltpu.VMEM((max(len(stages) - 1, 1),) + x.shape, x.dtype),
            pltpu.VMEM((slots,) + x.shape, x.dtype),
            pltpu.SemaphoreType.DMA((slots,)),
            pltpu.SemaphoreType.DMA((slots,)),
            pltpu.VMEM(faces.shape, faces.dtype),
            pltpu.SemaphoreType.DMA((6,)),
            pltpu.SemaphoreType.DMA((6,)),
        ],
        compiler_params=pltpu.CompilerParams(collective_id=3, has_side_effects=True),
    )(x, faces)


def faces_of(cells):
    return jnp.concatenate(
        [cells[-1], cells[0], cells[:, -1], cells[:, 0], cells[-1, :1], cells[0, -1:]], axis=0)


def padded_from(cells, halo):
    count_z, count_x = lax.axis_size("gz"), lax.axis_size("gx")
    z, x = lax.axis_index("gz"), lax.axis_index("gx")
    depth, width = cells.shape[1], cells.shape[0]
    low_z = jnp.where(z > 0, halo[:depth], 0.0)[None]
    high_z = jnp.where(z < count_z - 1, halo[depth:2 * depth], 0.0)[None]
    low_x = jnp.where(x > 0, halo[2 * depth:2 * depth + width], 0.0)[:, None]
    high_x = jnp.where(x < count_x - 1, halo[2 * depth + width:2 * depth + 2 * width], 0.0)[:, None]
    corner = 2 * depth + 2 * width
    low_z_high_x = jnp.where((z > 0) & (x < count_x - 1), halo[corner:corner + 1], 0.0)[None]
    high_z_low_x = jnp.where((z < count_z - 1) & (x > 0), halo[corner + 1:corner + 2], 0.0)[None]
    zero_line = jnp.zeros_like(cells[:1, :1])
    top = jnp.concatenate([zero_line, low_z, low_z_high_x], axis=1)
    middle = jnp.concatenate([low_x, cells, high_x], axis=1)
    bottom = jnp.concatenate([high_z_low_x, high_z, zero_line], axis=1)
    return jnp.concatenate([top, middle, bottom], axis=0)


def scalar_stages(n_gz, n_gx):
    stages = [("gz", 1, n_gz)]
    if n_gx % 4 == 0 and n_gx > 4:
        stages += [("gx", 1, 4), ("gx", 4, n_gx // 4)]
    else:
        stages += [("gx", 1, n_gx)]
    return [stage for stage in stages if stage[2] > 1]


def pack_pair(a, b):
    lane = lax.broadcasted_iota(jnp.int32, (8, 128), 1)
    return jnp.where(lane == 0, a, jnp.where(lane == 1, b, 0.0)).astype(jnp.float32)


def one_hot(index, size):
    return (index[:, None] == jnp.arange(size, dtype=jnp.int32)[None, :]).astype(jnp.bfloat16)


def block_apply_kernel(group, transposed, x_ref, blk_ref, w_ref, o_ref):
    o_ref[...] = jnp.zeros_like(o_ref)
    x = x_ref[...]
    chosen = blk_ref[...]
    zero = jnp.zeros_like(x)
    dims = (((1,), (1,)), ((), ())) if transposed else (((1,), (0,)), ((), ()))

    def step(p, carry):
        parts = [jnp.where(chosen == p * group + i, x, zero) for i in range(group)]
        joined = jnp.concatenate(parts, axis=1)
        weights = jnp.concatenate(
            [w_ref[p * group + i] for i in range(group)], axis=1 if transposed else 0)
        o_ref[...] += lax.dot_general(joined, weights, dims, preferred_element_type=jnp.float32)
        return carry

    lax.fori_loop(0, w_ref.shape[0] // group, step, 0)


def block_apply(x, chosen, weights, group, transposed):
    entries, width = x.shape
    flops = 2 * entries * width * width * weights.shape[0]
    return pl.pallas_call(
        functools.partial(block_apply_kernel, group, transposed),
        out_shape=jax.ShapeDtypeStruct((entries, width), jnp.float32),
        in_specs=[pl.BlockSpec(memory_space=pltpu.VMEM)] * 3,
        out_specs=pl.BlockSpec(memory_space=pltpu.VMEM),
        cost_estimate=pl.CostEstimate(
            flops=flops, transcendentals=0, bytes_accessed=weights.size * 2 + entries * width * 10),
    )(x, chosen, weights)


def shift_from(block, pairs_of):
    count_z, count_x = lax.axis_size("gz"), lax.axis_size("gx")
    pairs = []
    for z in range(count_z):
        for x in range(count_x):
            target = pairs_of(z, x)
            if 0 <= target[0] < count_z and 0 <= target[1] < count_x:
                pairs.append((z * count_x + x, target[0] * count_x + target[1]))
    return lax.ppermute(block, ("gz", "gx"), pairs)


def padded_2(cells):
    zero_line = jnp.zeros_like(cells[:1, :1])
    low_z = shift_from(cells[-1:], lambda z, x: (z + 1, x))
    high_z = shift_from(cells[:1], lambda z, x: (z - 1, x))
    low_x = shift_from(cells[:, -1:], lambda z, x: (z, x + 1))
    high_x = shift_from(cells[:, :1], lambda z, x: (z, x - 1))
    low_z_high_x = shift_from(cells[-1:, :1], lambda z, x: (z + 1, x - 1))
    high_z_low_x = shift_from(cells[:1, -1:], lambda z, x: (z - 1, x + 1))
    top = jnp.concatenate([zero_line, low_z, low_z_high_x], axis=1)
    middle = jnp.concatenate([low_x, cells, high_x], axis=1)
    bottom = jnp.concatenate([high_z_low_x, high_z, zero_line], axis=1)
    return jnp.concatenate([top, middle, bottom], axis=0)


def tv_grad(padded):
    base_cells = padded[:-1, :-1, :-1]
    diff_z = padded[1:, :-1, :-1] - base_cells
    diff_x = padded[:-1, 1:, :-1] - base_cells
    diff_y = padded[:-1, :-1, 1:] - base_cells
    inverse = lax.rsqrt(diff_z * diff_z + diff_x * diff_x + diff_y * diff_y + smooth_floor)
    flow_z = diff_z * inverse
    flow_x = diff_x * inverse
    flow_y = diff_y * inverse
    flow_all = flow_z + flow_x + flow_y
    return flow_z[:-1, 1:, 1:] + flow_x[1:, :-1, 1:] + flow_y[1:, 1:, :-1] - flow_all[1:, 1:, 1:]


def pad_depth(field):
    return jnp.pad(field, ((0, 0), (0, 0), (1, 1)))


def body(
    volume, measured, weight_blocks, view_order, tile_voxel, tile_column, tile_block, entry_count
):
    depth_z, depth_x, depth_y = volume.shape
    tiles_y = depth_y // group_rows
    tiles_u = measured.shape[2] // group_rows
    slab_tiles = depth_z * tiles_u
    plane_tiles = depth_x * tiles_y
    row_weight = jnp.sum(weight_blocks, axis=2, dtype=jnp.float32)
    col_weight = jnp.sum(weight_blocks, axis=1, dtype=jnp.float32)
    n_blocks = weight_blocks.shape[0]
    group = 4 if n_blocks % 4 == 0 else 1
    current = volume
    for turn_index in range(view_order.shape[0]):
        view_index = view_order[turn_index]
        voxel_list = lax.dynamic_index_in_dim(tile_voxel, view_index, 0, keepdims=False)[0]
        column_list = lax.dynamic_index_in_dim(tile_column, view_index, 0, keepdims=False)[0]
        block_list = lax.dynamic_index_in_dim(tile_block, view_index, 0, keepdims=False)[0]
        live_count = lax.dynamic_index_in_dim(entry_count, view_index, 0, keepdims=False)[0, 0]
        entries = voxel_list.shape[0]
        live = (jnp.arange(entries, dtype=jnp.int32) < live_count)[:, None]
        detector = voxel_list // plane_tiles * tiles_u + column_list
        voxel_tiles = current.astype(jnp.bfloat16).reshape(-1, group_rows)
        pick_voxel = one_hot(voxel_list, voxel_tiles.shape[0])
        pick_detector = one_hot(detector, slab_tiles)
        pick_block = jnp.where(live, one_hot(block_list, n_blocks), 0)
        blocks_column = block_list[:, None]

        cells = jnp.dot(pick_voxel, voxel_tiles, preferred_element_type=jnp.float32)
        product = block_apply(cells.astype(jnp.bfloat16), blocks_column, weight_blocks, group, True)
        product = jnp.where(live, product, 0.0)
        projection = lax.dot_general(
            pick_detector.astype(jnp.float32), product, (((0,), (0,)), ((), ())),
            precision=lax.Precision.HIGHEST)
        detector_blocks = lax.dot_general(
            pick_detector, pick_block, (((0,), (0,)), ((), ())), preferred_element_type=jnp.float32)
        ray_sum = jnp.dot(detector_blocks, row_weight, precision=lax.Precision.HIGHEST)
        target = lax.dynamic_index_in_dim(measured, view_index, 0, keepdims=False).reshape(
            slab_tiles, group_rows
        )
        n_gx = lax.axis_size("gx")
        joined = jnp.concatenate([projection, ray_sum], axis=1).astype(jnp.bfloat16)
        joined = vector_sum(joined.reshape(n_gx, slab_tiles // n_gx, 2 * group_rows))
        joined = joined.reshape(slab_tiles, 2 * group_rows).astype(jnp.float32)
        projection, ray_sum = joined[:, :group_rows], joined[:, group_rows:]
        residual = ((target - projection) / (ray_sum + 1.0)).astype(jnp.bfloat16)

        pixels = jnp.dot(pick_detector, residual, preferred_element_type=jnp.float32)
        product = block_apply(pixels.astype(jnp.bfloat16), blocks_column, weight_blocks, group, False)
        product = jnp.where(live, product, 0.0)
        change = lax.dot_general(
            pick_voxel.astype(jnp.float32), product, (((0,), (0,)), ((), ())),
            precision=lax.Precision.HIGHEST)
        voxel_blocks = lax.dot_general(
            pick_voxel, pick_block, (((0,), (0,)), ((), ())), preferred_element_type=jnp.float32)
        voxel_sum = jnp.dot(voxel_blocks, col_weight, precision=lax.Precision.HIGHEST)
        current = current + (change / (voxel_sum + 1.0)).reshape(current.shape)
    art_volume = jnp.maximum(current, 0.0)
    difference = art_volume - volume
    change_part = jnp.sum(difference * difference)
    stages = scalar_stages(lax.axis_size("gz"), lax.axis_size("gx"))
    totals, halo = tv_exchange(pack_pair(0.0, change_part), art_volume, stages)
    change_total = totals[0, 1]
    padded = padded_from(art_volume, halo)
    smooth = art_volume
    for sweep_index in range(TV_STEPS):
        slope = tv_grad(pad_depth(padded))
        slope_part = jnp.sum(slope * slope)
        totals, halo = tv_exchange(pack_pair(slope_part, 0.0), slope, stages)
        slope_total = totals[0, 0]
        scale_now = step_gain * jnp.sqrt(change_total) / jnp.sqrt(slope_total + norm_floor)
        smooth = smooth - scale_now * slope
        if sweep_index + 1 < TV_STEPS:
            padded = padded - scale_now * padded_from(slope, halo)
    return smooth


def solution(mesh):
    return jax.shard_map(
        body,
        mesh=mesh,
        in_specs=(
            P("gz", "gx", None),
            P(None, "gz", None),
            P(),
            P(),
            P(None, "gz", "gx"),
            P(None, "gz", "gx"),
            P(None, "gz", "gx"),
            P(None, "gz", "gx"),
        ),
        out_specs=P("gz", "gx", None),
        check_vma=False,
    )
```

profile of v0, /device:TPU:1, one launch (start us, length us, event | category | flops | bytes accessed | tf_op | source)
XLA Modules:
  0.0 288.7 jit_solution(751088162010649999)
XLA Ops:
  10.3 2.2 convert_reduce_fusion.1
  17.6 10.5 %shard_map.82 = f32[512,128]{1,0:T(8,128)} custom-call(bf16[512,128]{1,0:T(8,128)(2,1)} %fusion.8.x_ref, s32[512,1]{1,0:T(8,128)} %copy.36.blk_ref, bf16[64,128,128]{2,1,0:T(8,128)(2,1)} %w_ref.7), custom_call_target="tpu_custom_call" | custom-call | flops 1073741824 | bytes 2752512 | tf_op jit(solution)/shard_map/pallas_call | solution.py:286
  28.1 2.1 convolution_convert_fusion.3
  30.9 28.7 %shard_map.83 = bf16[32,16,256]{2,1,0:T(8,128)(2,1)} custom-call(bf16[32,16,256]{2,1,0:T(8,128)(2,1)} %pad_maximum_fusion.1.x_ref), custom_call_target="tpu_custom_call" | custom-call | tf_op jit(solution)/shard_map/pallas_call | solution.py:64
  64.9 10.1 %shard_map.84 = f32[512,128]{1,0:T(8,128)} custom-call(bf16[512,128]{1,0:T(8,128)(2,1)} %convolution_convert_fusion.2.x_ref, s32[512,1]{1,0:T(8,128)} %copy.36.blk_ref, bf16[64,128,128]{2,1,0:T(8,128)(2,1)} %w_ref.7), custom_call_target="tpu_custom_call" | custom-call | flops 1073741824 | bytes 2752512 | tf_op jit(solution)/shard_map/pallas_call | solution.py:286
  75.0 2.9 %fusion.6 = f32[1024,128]{1,0:T(8,128)S(1)} fusion(f32[1024,128]{1,0:T(8,128)S(1)} %convolution_add_fusion.1, s32[512]{0:T(512)S(1)} %bitcast.190, f32[512,128]{1,0:T(8,128)} %shard_map.84, pred[512]{0:T(512)(128)(4,1)S(1)} %iota_compare_fusion.27), kind=kOutput, calls=%fused_computation.26 | convolution fusion | flops 806027264 | bytes 1313280 | tf_op jit(solution)/shard_map/dot_general | solution.py:388
  80.0 20.8 %shard_map.85 = f32[512,128]{1,0:T(8,128)} custom-call(bf16[512,128]{1,0:T(8,128)(2,1)} %fusion.9.x_ref, s32[512,1]{1,0:T(8,128)} %copy.42.blk_ref, bf16[64,128,128]{2,1,0:T(8,128)(2,1)} %w_ref.7), custom_call_target="tpu_custom_call" | custom-call | flops 1073741824 | bytes 2752512 | tf_op jit(solution)/shard_map/pallas_call | solution.py:286
  100.9 2.1 convolution_convert_fusion.1
  103.7 22.9 %shard_map.86 = bf16[32,16,256]{2,1,0:T(8,128)(2,1)} custom-call(bf16[32,16,256]{2,1,0:T(8,128)(2,1)} %pad_maximum_fusion.2.x_ref), custom_call_target="tpu_custom_call" | custom-call | tf_op jit(solution)/shard_map/pallas_call | solution.py:64
  128.7 10.1 %shard_map.87 = f32[512,128]{1,0:T(8,128)} custom-call(bf16[512,128]{1,0:T(8,128)(2,1)} %convolution_convert_fusion.x_ref, s32[512,1]{1,0:T(8,128)} %copy.42.blk_ref, bf16[64,128,128]{2,1,0:T(8,128)(2,1)} %w_ref.7), custom_call_target="tpu_custom_call" | custom-call | flops 1073741824 | bytes 2752512 | tf_op jit(solution)/shard_map/pallas_call | solution.py:286
  138.8 2.9 %fusion.7 = f32[1024,128]{1,0:T(8,128)S(1)} fusion(f32[1024,128]{1,0:T(8,128)S(1)} %convolution_add_fusion, s32[512]{0:T(512)S(1)} %bitcast.186, f32[512,128]{1,0:T(8,128)} %shard_map.87, pred[512]{0:T(512)(128)(4,1)S(1)} %iota_compare_fusion.26), kind=kOutput, calls=%fused_computation.27 | convolution fusion | flops 806027264 | bytes 1313280 | tf_op jit(solution)/shard_map/dot_general | solution.py:388
  144.7 3.1 %concatenate.81.f_ref = f32[98,256]{1,0:T(8,128)} concatenate(f32[16,256]{1,0:T(8,128)S(1)} %bitcast.172, f32[16,256]{1,0:T(8,128)S(1)} %bitcast.167, f32[32,256]{1,0:T(8,128)S(1)} %get-tuple-element.78, f32[32,256]{1,0:T(8,128)S(1)} %get-tuple-element.77, f32[1,256]{1,0:T(1,128)S(1)} %get-tuple-element.76, f32[1,256]{1,0:T(1,128)S(1)} %get-tuple-element.75), dimensions={0} | concatenate | bytes 200704 | tf_op jit(solution)/shard_map/concatenate | solution.py:225
  147.7 19.8 %shard_map.88 = (f32[8,128]{1,0:T(8,128)}, f32[98,256]{1,0:T(8,128)}) custom-call(f32[8,128]{1,0:T(8,128)} %broadcast_select_fusion.x_ref, f32[98,256]{1,0:T(8,128)} %concatenate.81.f_ref), custom_call_target="tpu_custom_call" | custom-call | tf_op jit(solution)/shard_map/pallas_call | solution.py:206
  174.2 1.5 multiply_reduce_fusion.3
  177.0 3.1 %concatenate.86.f_ref = f32[98,256]{1,0:T(8,128)} concatenate(f32[16,256]{1,0:T(8,128)S(1)} %bitcast.173, f32[16,256]{1,0:T(8,128)S(1)} %bitcast.168, f32[32,256]{1,0:T(8,128)S(1)} %get-tuple-element.72, f32[32,256]{1,0:T(8,128)S(1)} %get-tuple-element.71, f32[1,256]{1,0:T(1,128)S(1)} %get-tuple-element.70, f32[1,256]{1,0:T(1,128)S(1)} %get-tuple-element.69), dimensions={0} | concatenate | bytes 200704 | tf_op jit(solution)/shard_map/concatenate | solution.py:225
  180.1 16.5 %shard_map.89 = (f32[8,128]{1,0:T(8,128)}, f32[98,256]{1,0:T(8,128)}) custom-call(f32[8,128]{1,0:T(8,128)} %iota.65.x_ref, f32[98,256]{1,0:T(8,128)} %concatenate.86.f_ref), custom_call_target="tpu_custom_call" | custom-call | tf_op jit(solution)/shard_map/pallas_call | solution.py:206
  203.4 1.5 multiply_reduce_fusion.2
  206.2 3.1 %concatenate.91.f_ref = f32[98,256]{1,0:T(8,128)} concatenate(f32[16,256]{1,0:T(8,128)S(1)} %bitcast.174, f32[16,256]{1,0:T(8,128)S(1)} %bitcast.169, f32[32,256]{1,0:T(8,128)S(1)} %get-tuple-element.66, f32[32,256]{1,0:T(8,128)S(1)} %get-tuple-element.65, f32[1,256]{1,0:T(1,128)S(1)} %get-tuple-element.64, f32[1,256]{1,0:T(1,128)S(1)} %get-tuple-element.63), dimensions={0} | concatenate | bytes 200704 | tf_op jit(solution)/shard_map/concatenate | solution.py:225
  209.2 17.0 %shard_map.90 = (f32[8,128]{1,0:T(8,128)}, f32[98,256]{1,0:T(8,128)}) custom-call(f32[8,128]{1,0:T(8,128)} %iota.66.x_ref, f32[98,256]{1,0:T(8,128)} %concatenate.91.f_ref), custom_call_target="tpu_custom_call" | custom-call | tf_op jit(solution)/shard_map/pallas_call | solution.py:206
  233.2 1.5 multiply_reduce_fusion.1
  236.1 3.1 %concatenate.96.f_ref = f32[98,256]{1,0:T(8,128)} concatenate(f32[16,256]{1,0:T(8,128)S(1)} %bitcast.175, f32[16,256]{1,0:T(8,128)S(1)} %bitcast.170, f32[32,256]{1,0:T(8,128)S(1)} %get-tuple-element.60, f32[32,256]{1,0:T(8,128)S(1)} %get-tuple-element.59, f32[1,256]{1,0:T(1,128)S(1)} %get-tuple-element.58, f32[1,256]{1,0:T(1,128)S(1)} %get-tuple-element.57), dimensions={0} | concatenate | bytes 200704 | tf_op jit(solution)/shard_map/concatenate | solution.py:225
  239.1 16.6 %shard_map.91 = (f32[8,128]{1,0:T(8,128)}, f32[98,256]{1,0:T(8,128)}) custom-call(f32[8,128]{1,0:T(8,128)} %iota.67.x_ref, f32[98,256]{1,0:T(8,128)} %concatenate.96.f_ref), custom_call_target="tpu_custom_call" | custom-call | tf_op jit(solution)/shard_map/pallas_call | solution.py:206
  265.2 3.1 %concatenate.101.f_ref = f32[98,256]{1,0:T(8,128)} concatenate(f32[16,256]{1,0:T(8,128)S(1)} %bitcast.176, f32[16,256]{1,0:T(8,128)S(1)} %bitcast.171, f32[32,256]{1,0:T(8,128)S(1)} %get-tuple-element.54, f32[32,256]{1,0:T(8,128)S(1)} %get-tuple-element.53, f32[1,256]{1,0:T(1,128)S(1)} %get-tuple-element.52, f32[1,256]{1,0:T(1,128)S(1)} %get-tuple-element.51), dimensions={0} | concatenate | bytes 200704 | tf_op jit(solution)/shard_map/concatenate | solution.py:225
  268.3 17.0 %shard_map.92 = (f32[8,128]{1,0:T(8,128)}, f32[98,256]{1,0:T(8,128)}) custom-call(f32[8,128]{1,0:T(8,128)} %iota.68.x_ref, f32[98,256]{1,0:T(8,128)} %concatenate.101.f_ref), custom_call_target="tpu_custom_call" | custom-call | tf_op jit(solution)/shard_map/pallas_call | solution.py:206
  (123 shorter events, 58.4 us)
Async XLA Ops:
  14.2 2.1 copy-start
  62.2 1.5 copy-start.1
where the time goes:
time: 294 us; the launch traced here: 289 us
  Pallas kernels  190 us (65%)
  other arithmetic  38.5 us (13%)
  local copies, waits for them, and re-layouts  32.5 us (11%)
  matrix products  19.4 us (7%)
  between operations  8.31 us (3%)
    pallas_call x5, Pallas kernels, tv_exchange(): pl.pallas_call(functools.partial(tv_exchange_kernel, stages, (cells.shape...  86.8 us
    pallas_call x2, Pallas kernels, vector_sum(): pl.pallas_call(functools.partial(vector_sum_kernel, n), out_shape=jax.Sha...  51.7 us
    pallas_call x4, Pallas kernels, block_apply(): pl.pallas_call(functools.partial(block_apply_kernel, group, transposed),...  51.5 us
    concatenate x5, local copies, waits for them, and re-layouts, faces_of(): jnp.concatenate([cells[-1], cells[0], cells[:, -1], cells[:, 0], cells[-1...  15.3 us
    reduce_sum x4, other arithmetic, body(): slope_part = jnp.sum(slope * slope)  5.95 us

commit v1 on v0

--- a/solution.py
+++ b/solution.py
@@ -1,4 +1,5 @@
 import functools
+import math
 
 import jax
 import jax.numpy as jnp
@@ -80,62 +81,25 @@
 
 
 def _stage_peers(stage):
-    axis, stride, size = stage
-    index = lax.axis_index(axis)
-    position = lax.rem(index // stride, size)
-    base = index - position * stride
-    return [base + lax.rem(position + d, size) * stride for d in range(1, size)]
-
-
-def scalar_sum_kernel(stages, x_ref, o_ref, buf, recv, ssem, rsem):
-    barrier = pltpu.get_barrier_semaphore()
-    count = 0
-    for stage in stages:
-        for peer in _stage_peers(stage):
-            pl.semaphore_signal(barrier, inc=1, device_id=_peer(stage[0], peer), device_id_type=MESH)
-            count += 1
-    pl.semaphore_wait(barrier, count)
-    total = x_ref[...]
-    slot = 0
-    for s, stage in enumerate(stages):
-        axis, stride, size = stage
-        position = lax.rem(lax.axis_index(axis) // stride, size)
-        source = x_ref if s == 0 else buf.at[s - 1]
-        recv[slot] = total
-        sends = []
-        for d, peer in enumerate(_stage_peers(stage), start=1):
-            copy = pltpu.make_async_remote_copy(
-                src_ref=source, dst_ref=recv.at[slot + d], send_sem=ssem.at[slot + d],
-                recv_sem=rsem.at[slot + d], device_id=_peer(axis, peer), device_id_type=MESH)
-            copy.start()
-            sends.append(copy)
-        for copy in sends:
-            copy.wait()
-        total = recv[slot + position]
-        for p in range(1, size):
-            total = total + recv[slot + lax.rem(position - p + size, size)]
-        slot += size
-        if s + 1 < len(stages):
-            buf[s] = total
-    o_ref[...] = total
-
-
-def scalar_sum(x, stages):
-    slots = sum(size for _, _, size in stages)
-    return pl.pallas_call(
-        functools.partial(scalar_sum_kernel, stages),
-        out_shape=jax.ShapeDtypeStruct(x.shape, x.dtype),
-        in_specs=[pl.BlockSpec(memory_space=pltpu.VMEM)],
-        out_specs=pl.BlockSpec(memory_space=pltpu.VMEM),
-        scratch_shapes=[
-            pltpu.VMEM((max(len(stages) - 1, 1),) + x.shape, x.dtype),
-            pltpu.VMEM((slots,) + x.shape, x.dtype),
-            pltpu.SemaphoreType.DMA((slots,)),
-            pltpu.SemaphoreType.DMA((slots,)),
-        ],
-        cost_estimate=pl.CostEstimate(flops=0, transcendentals=0, bytes_accessed=40_000_000),
-        compiler_params=pltpu.CompilerParams(collective_id=2, has_side_effects=True),
-    )(x)
+    if isinstance(stage[0], str):
+        stage = [stage]
+    index = {axis: lax.axis_index(axis) for axis, _, _ in stage}
+    digits = [lax.rem(index[axis] // stride, size) for axis, stride, size in stage]
+    total = 1
+    position = 0
+    for (_, _, size), digit in zip(stage, digits):
+        position = position * size + digit
+        total *= size
+    peers = []
+    for d in range(1, total):
+        q = lax.rem(position + d, total)
+        coords = dict(index)
+        rest = total
+        for (axis, stride, size), digit in zip(stage, digits):
+            rest //= size
+            coords[axis] = coords[axis] + (lax.rem(q // rest, size) - digit) * stride
+        peers.append((coords.get("gz", lax.axis_index("gz")), coords.get("gx", lax.axis_index("gx"))))
+    return position, total, peers
 
 
 def halo_routes(depth, width):
@@ -155,11 +119,12 @@
 
 def tv_exchange_kernel(stages, shape, x_ref, f_ref, o_ref, h_ref, buf, recv, ssem, rsem, hrecv, hsend, hget):
     routes = halo_routes(*shape)
+    plan = [_stage_peers(stage) for stage in stages]
     barrier = pltpu.get_barrier_semaphore()
     count = 0
-    for stage in stages:
-        for peer in _stage_peers(stage):
-            pl.semaphore_signal(barrier, inc=1, device_id=_peer(stage[0], peer), device_id_type=MESH)
+    for _, _, peers in plan:
+        for peer in peers:
+            pl.semaphore_signal(barrier, inc=1, device_id=peer, device_id_type=MESH)
             count += 1
     for _, _, target in routes:
         pl.semaphore_signal(barrier, inc=1, device_id=target, device_id_type=MESH)
@@ -174,16 +139,14 @@
         halo.append(copy)
     total = x_ref[...]
     slot = 0
-    for s, stage in enumerate(stages):
-        axis, stride, size = stage
-        position = lax.rem(lax.axis_index(axis) // stride, size)
+    for s, (position, size, peers) in enumerate(plan):
         source = x_ref if s == 0 else buf.at[s - 1]
         recv[slot] = total
         sends = []
-        for d, peer in enumerate(_stage_peers(stage), start=1):
+        for d, peer in enumerate(peers, start=1):
             copy = pltpu.make_async_remote_copy(
                 src_ref=source, dst_ref=recv.at[slot + d], send_sem=ssem.at[slot + d],
-                recv_sem=rsem.at[slot + d], device_id=_peer(axis, peer), device_id_type=MESH)
+                recv_sem=rsem.at[slot + d], device_id=peer, device_id_type=MESH)
             copy.start()
             sends.append(copy)
         for copy in sends:
@@ -192,7 +155,7 @@
         for p in range(1, size):
             total = total + recv[slot + lax.rem(position - p + size, size)]
         slot += size
-        if s + 1 < len(stages):
+        if s + 1 < len(plan):
             buf[s] = total
     o_ref[...] = total
     for copy in halo:
@@ -202,7 +165,7 @@
 
 def tv_exchange(x, cells, stages):
     faces = faces_of(cells)
-    slots = sum(size for _, _, size in stages)
+    slots = sum(math.prod(size for _, _, size in stage) for stage in stages)
     return pl.pallas_call(
         functools.partial(tv_exchange_kernel, stages, (cells.shape[1], cells.shape[0])),
         out_shape=(jax.ShapeDtypeStruct(x.shape, x.dtype), jax.ShapeDtypeStruct(faces.shape, faces.dtype)),
@@ -245,12 +208,9 @@
 
 
 def scalar_stages(n_gz, n_gx):
-    stages = [("gz", 1, n_gz)]
     if n_gx % 4 == 0 and n_gx > 4:
-        stages += [("gx", 1, 4), ("gx", 4, n_gx // 4)]
-    else:
-        stages += [("gx", 1, n_gx)]
-    return [stage for stage in stages if stage[2] > 1]
+        return [[("gz", 1, n_gz), ("gx", 1, 4)], [("gx", 4, n_gx // 4)]]
+    return [[("gz", 1, n_gz)], [("gx", 1, n_gx)]]
 
 
 def pack_pair(a, b):

time: 294 us -> 279 us (0.949)
  Pallas kernels: 190 us -> 175 us
    pallas_call x4, Pallas kernels: 51.5 us -> 41 us  [block_apply(): pl.pallas_call(functools.partial(block_apply_kernel, group, transposed),...]
    pallas_call x5, Pallas kernels: 86.8 us -> 82 us  [tv_exchange(): pl.pallas_call(functools.partial(tv_exchange_kernel, stages, (cells.shape...]
where the time goes in v1:
time: 279 us; the launch traced here: 273 us
  Pallas kernels  175 us (63%)
  other arithmetic  38.5 us (14%)
  local copies, waits for them, and re-layouts  32.5 us (12%)
  matrix products  19.4 us (7%)
  between operations  8.3 us (3%)
    pallas_call x5, Pallas kernels, tv_exchange(): pl.pallas_call(functools.partial(tv_exchange_kernel, stages, (cells.shape...  82 us
    pallas_call x2, Pallas kernels, vector_sum(): pl.pallas_call(functools.partial(vector_sum_kernel, n), out_shape=jax.Sha...  51.7 us
    pallas_call x4, Pallas kernels, block_apply(): pl.pallas_call(functools.partial(block_apply_kernel, group, transposed),...  41 us
    concatenate x5, local copies, waits for them, and re-layouts, faces_of(): jnp.concatenate([cells[-1], cells[0], cells[:, -1], cells[:, 0], cells[-1...  15.3 us
    reduce_sum x4, other arithmetic, body(): slope_part = jnp.sum(slope * slope)  6.16 us
    dot_general x2, matrix products, body(): lax.dot_general(pick_voxel.astype(jnp.float32), product, (((0,), (0,)), (...  5.83 us
    mul x4, other arithmetic, tv_grad(): flow_z = diff_z * inverse  5.69 us

profile of v1, /device:TPU:1, one launch (start us, length us, event | category | flops | bytes accessed | tf_op | source)
XLA Modules:
  0.0 273.5 jit_solution(16352661063164887974)
XLA Ops:
  10.3 2.2 convert_reduce_fusion.1
  17.6 10.5 %shard_map.82 = f32[512,128]{1,0:T(8,128)} custom-call(bf16[512,128]{1,0:T(8,128)(2,1)} %fusion.8.x_ref, s32[512,1]{1,0:T(8,128)} %copy.36.blk_ref, bf16[64,128,128]{2,1,0:T(8,128)(2,1)} %w_ref.7), custom_call_target="tpu_custom_call" | custom-call | flops 1073741824 | bytes 2752512 | tf_op jit(solution)/shard_map/pallas_call | solution.py:246
  28.2 2.1 convolution_convert_fusion.3
  31.0 28.7 %shard_map.83 = bf16[32,16,256]{2,1,0:T(8,128)(2,1)} custom-call(bf16[32,16,256]{2,1,0:T(8,128)(2,1)} %pad_maximum_fusion.1.x_ref), custom_call_target="tpu_custom_call" | custom-call | tf_op jit(solution)/shard_map/pallas_call | solution.py:65
  65.0 10.1 %shard_map.84 = f32[512,128]{1,0:T(8,128)} custom-call(bf16[512,128]{1,0:T(8,128)(2,1)} %convolution_convert_fusion.2.x_ref, s32[512,1]{1,0:T(8,128)} %copy.36.blk_ref, bf16[64,128,128]{2,1,0:T(8,128)(2,1)} %w_ref.7), custom_call_target="tpu_custom_call" | custom-call | flops 1073741824 | bytes 2752512 | tf_op jit(solution)/shard_map/pallas_call | solution.py:246
  75.0 2.9 %fusion.6 = f32[1024,128]{1,0:T(8,128)S(1)} fusion(f32[1024,128]{1,0:T(8,128)S(1)} %convolution_add_fusion.1, s32[512]{0:T(512)S(1)} %bitcast.190, f32[512,128]{1,0:T(8,128)} %shard_map.84, pred[512]{0:T(512)(128)(4,1)S(1)} %iota_compare_fusion.27), kind=kOutput, calls=%fused_computation.26 | convolution fusion | flops 806027264 | bytes 1313280 | tf_op jit(solution)/shard_map/dot_general | solution.py:348
  80.1 10.2 %shard_map.85 = f32[512,128]{1,0:T(8,128)} custom-call(bf16[512,128]{1,0:T(8,128)(2,1)} %fusion.9.x_ref, s32[512,1]{1,0:T(8,128)} %copy.42.blk_ref, bf16[64,128,128]{2,1,0:T(8,128)(2,1)} %w_ref.7), custom_call_target="tpu_custom_call" | custom-call | flops 1073741824 | bytes 2752512 | tf_op jit(solution)/shard_map/pallas_call | solution.py:246
  90.4 2.1 convolution_convert_fusion.1
  93.2 23.0 %shard_map.86 = bf16[32,16,256]{2,1,0:T(8,128)(2,1)} custom-call(bf16[32,16,256]{2,1,0:T(8,128)(2,1)} %pad_maximum_fusion.2.x_ref), custom_call_target="tpu_custom_call" | custom-call | tf_op jit(solution)/shard_map/pallas_call | solution.py:65
  118.2 10.1 %shard_map.87 = f32[512,128]{1,0:T(8,128)} custom-call(bf16[512,128]{1,0:T(8,128)(2,1)} %convolution_convert_fusion.x_ref, s32[512,1]{1,0:T(8,128)} %copy.42.blk_ref, bf16[64,128,128]{2,1,0:T(8,128)(2,1)} %w_ref.7), custom_call_target="tpu_custom_call" | custom-call | flops 1073741824 | bytes 2752512 | tf_op jit(solution)/shard_map/pallas_call | solution.py:246
  128.3 2.9 %fusion.7 = f32[1024,128]{1,0:T(8,128)S(1)} fusion(f32[1024,128]{1,0:T(8,128)S(1)} %convolution_add_fusion, s32[512]{0:T(512)S(1)} %bitcast.186, f32[512,128]{1,0:T(8,128)} %shard_map.87, pred[512]{0:T(512)(128)(4,1)S(1)} %iota_compare_fusion.26), kind=kOutput, calls=%fused_computation.27 | convolution fusion | flops 806027264 | bytes 1313280 | tf_op jit(solution)/shard_map/dot_general | solution.py:348
  134.2 3.1 %concatenate.81.f_ref = f32[98,256]{1,0:T(8,128)} concatenate(f32[16,256]{1,0:T(8,128)S(1)} %bitcast.172, f32[16,256]{1,0:T(8,128)S(1)} %bitcast.167, f32[32,256]{1,0:T(8,128)S(1)} %get-tuple-element.78, f32[32,256]{1,0:T(8,128)S(1)} %get-tuple-element.77, f32[1,256]{1,0:T(1,128)S(1)} %get-tuple-element.76, f32[1,256]{1,0:T(1,128)S(1)} %get-tuple-element.75), dimensions={0} | concatenate | bytes 200704 | tf_op jit(solution)/shard_map/concatenate | solution.py:188
  137.2 19.2 %shard_map.88 = (f32[8,128]{1,0:T(8,128)}, f32[98,256]{1,0:T(8,128)}) custom-call(f32[8,128]{1,0:T(8,128)} %broadcast_select_fusion.x_ref, f32[98,256]{1,0:T(8,128)} %concatenate.81.f_ref), custom_call_target="tpu_custom_call" | custom-call | tf_op jit(solution)/shard_map/pallas_call | solution.py:169
  163.2 1.5 multiply_reduce_fusion.3
  166.0 3.1 %concatenate.86.f_ref = f32[98,256]{1,0:T(8,128)} concatenate(f32[16,256]{1,0:T(8,128)S(1)} %bitcast.173, f32[16,256]{1,0:T(8,128)S(1)} %bitcast.168, f32[32,256]{1,0:T(8,128)S(1)} %get-tuple-element.72, f32[32,256]{1,0:T(8,128)S(1)} %get-tuple-element.71, f32[1,256]{1,0:T(1,128)S(1)} %get-tuple-element.70, f32[1,256]{1,0:T(1,128)S(1)} %get-tuple-element.69), dimensions={0} | concatenate | bytes 200704 | tf_op jit(solution)/shard_map/concatenate | solution.py:188
  169.1 15.4 %shard_map.89 = (f32[8,128]{1,0:T(8,128)}, f32[98,256]{1,0:T(8,128)}) custom-call(f32[8,128]{1,0:T(8,128)} %iota.65.x_ref, f32[98,256]{1,0:T(8,128)} %concatenate.86.f_ref), custom_call_target="tpu_custom_call" | custom-call | tf_op jit(solution)/shard_map/pallas_call | solution.py:169
  191.3 1.7 multiply_reduce_fusion.2
  194.3 3.1 %concatenate.91.f_ref = f32[98,256]{1,0:T(8,128)} concatenate(f32[16,256]{1,0:T(8,128)S(1)} %bitcast.174, f32[16,256]{1,0:T(8,128)S(1)} %bitcast.169, f32[32,256]{1,0:T(8,128)S(1)} %get-tuple-element.66, f32[32,256]{1,0:T(8,128)S(1)} %get-tuple-element.65, f32[1,256]{1,0:T(1,128)S(1)} %get-tuple-element.64, f32[1,256]{1,0:T(1,128)S(1)} %get-tuple-element.63), dimensions={0} | concatenate | bytes 200704 | tf_op jit(solution)/shard_map/concatenate | solution.py:188
  197.4 16.0 %shard_map.90 = (f32[8,128]{1,0:T(8,128)}, f32[98,256]{1,0:T(8,128)}) custom-call(f32[8,128]{1,0:T(8,128)} %iota.66.x_ref, f32[98,256]{1,0:T(8,128)} %concatenate.91.f_ref), custom_call_target="tpu_custom_call" | custom-call | tf_op jit(solution)/shard_map/pallas_call | solution.py:169
  220.1 1.5 multiply_reduce_fusion.1
  223.0 3.1 %concatenate.96.f_ref = f32[98,256]{1,0:T(8,128)} concatenate(f32[16,256]{1,0:T(8,128)S(1)} %bitcast.175, f32[16,256]{1,0:T(8,128)S(1)} %bitcast.170, f32[32,256]{1,0:T(8,128)S(1)} %get-tuple-element.60, f32[32,256]{1,0:T(8,128)S(1)} %get-tuple-element.59, f32[1,256]{1,0:T(1,128)S(1)} %get-tuple-element.58, f32[1,256]{1,0:T(1,128)S(1)} %get-tuple-element.57), dimensions={0} | concatenate | bytes 200704 | tf_op jit(solution)/shard_map/concatenate | solution.py:188
  226.0 15.7 %shard_map.91 = (f32[8,128]{1,0:T(8,128)}, f32[98,256]{1,0:T(8,128)}) custom-call(f32[8,128]{1,0:T(8,128)} %iota.67.x_ref, f32[98,256]{1,0:T(8,128)} %concatenate.96.f_ref), custom_call_target="tpu_custom_call" | custom-call | tf_op jit(solution)/shard_map/pallas_call | solution.py:169
  251.3 3.1 %concatenate.101.f_ref = f32[98,256]{1,0:T(8,128)} concatenate(f32[16,256]{1,0:T(8,128)S(1)} %bitcast.176, f32[16,256]{1,0:T(8,128)S(1)} %bitcast.171, f32[32,256]{1,0:T(8,128)S(1)} %get-tuple-element.54, f32[32,256]{1,0:T(8,128)S(1)} %get-tuple-element.53, f32[1,256]{1,0:T(1,128)S(1)} %get-tuple-element.52, f32[1,256]{1,0:T(1,128)S(1)} %get-tuple-element.51), dimensions={0} | concatenate | bytes 200704 | tf_op jit(solution)/shard_map/concatenate | solution.py:188
  254.3 15.7 %shard_map.92 = (f32[8,128]{1,0:T(8,128)}, f32[98,256]{1,0:T(8,128)}) custom-call(f32[8,128]{1,0:T(8,128)} %iota.68.x_ref, f32[98,256]{1,0:T(8,128)} %concatenate.101.f_ref), custom_call_target="tpu_custom_call" | custom-call | tf_op jit(solution)/shard_map/pallas_call | solution.py:169
  (123 shorter events, 58.2 us)
Async XLA Ops:
  14.2 2.1 copy-start
  62.2 1.5 copy-start.1

commit v2 on v1

--- a/solution.py
+++ b/solution.py
@@ -32,30 +32,39 @@
     for d in range(1, n):
         pl.semaphore_signal(barrier, inc=1, device_id=_peer("gx", lax.rem(me + d, n)), device_id_type=MESH)
     pl.semaphore_wait(barrier, n - 1)
-    sends = []
-    for d in range(1, n):
+
+    def scatter_copy(d):
         dst = lax.rem(me + d, n)
-        copy = pltpu.make_async_remote_copy(
+        return pltpu.make_async_remote_copy(
             src_ref=x_ref.at[dst], dst_ref=recv.at[d], send_sem=ssem1.at[d], recv_sem=rsem1.at[d],
             device_id=_peer("gx", dst), device_id_type=MESH)
-        copy.start()
-        sends.append(copy)
-    for copy in sends:
-        copy.wait()
-    total = x_ref[me].astype(jnp.float32)
-    for d in range(1, n):
-        total = total + recv[d].astype(jnp.float32)
-    red[...] = total.astype(red.dtype)
-    sends = []
-    for d in range(1, n):
+
+    def gather_copy(d):
         dst = lax.rem(me + d, n)
-        copy = pltpu.make_async_remote_copy(
+        return pltpu.make_async_remote_copy(
             src_ref=red, dst_ref=gath.at[me], send_sem=ssem2.at[d], recv_sem=rsem2.at[d],
             device_id=_peer("gx", dst), device_id_type=MESH)
-        copy.start()
-        sends.append(copy)
-    for copy in sends:
-        copy.wait()
+
+    @pl.loop(1, n)
+    def _(d):
+        scatter_copy(d).start()
+
+    @pl.loop(1, n)
+    def _(d):
+        scatter_copy(d).wait()
+
+    total = lax.fori_loop(
+        1, n, lambda d, acc: acc + recv[d].astype(jnp.float32), x_ref[me].astype(jnp.float32))
+    red[...] = total.astype(red.dtype)
+
+    @pl.loop(1, n)
+    def _(d):
+        gather_copy(d).start()
+
+    @pl.loop(1, n)
+    def _(d):
+        gather_copy(d).wait()
+
     gath[me] = red[...]
     o_ref[...] = gath[...]
 
@@ -184,6 +193,40 @@
     )(x, faces)
 
 
+def halo_exchange_kernel(shape, f_ref, h_ref, hrecv, hsend, hget):
+    routes = halo_routes(*shape)
+    barrier = pltpu.get_barrier_semaphore()
+    for _, _, target in routes:
+        pl.semaphore_signal(barrier, inc=1, device_id=target, device_id_type=MESH)
+    pl.semaphore_wait(barrier, len(routes))
+    halo = []
+    for k, (row, rows, target) in enumerate(routes):
+        copy = pltpu.make_async_remote_copy(
+            src_ref=f_ref.at[pl.ds(row, rows)], dst_ref=hrecv.at[pl.ds(row, rows)],
+            send_sem=hsend.at[k], recv_sem=hget.at[k], device_id=target, device_id_type=MESH)
+        copy.start()
+        halo.append(copy)
+    for copy in halo:
+        copy.wait()
+    h_ref[...] = hrecv[...]
+
+
+def halo_exchange(cells):
+    faces = faces_of(cells)
+    return pl.pallas_call(
+        functools.partial(halo_exchange_kernel, (cells.shape[1], cells.shape[0])),
+        out_shape=jax.ShapeDtypeStruct(faces.shape, faces.dtype),
+        in_specs=[pl.BlockSpec(memory_space=pltpu.VMEM)],
+        out_specs=pl.BlockSpec(memory_space=pltpu.VMEM),
+        scratch_shapes=[
+            pltpu.VMEM(faces.shape, faces.dtype),
+            pltpu.SemaphoreType.DMA((6,)),
+            pltpu.SemaphoreType.DMA((6,)),
+        ],
+        compiler_params=pltpu.CompilerParams(collective_id=4, has_side_effects=True),
+    )(faces)
+
+
 def faces_of(cells):
     return jnp.concatenate(
         [cells[-1], cells[0], cells[:, -1], cells[:, 0], cells[-1, :1], cells[0, -1:]], axis=0)
@@ -356,14 +399,16 @@
     difference = art_volume - volume
     change_part = jnp.sum(difference * difference)
     stages = scalar_stages(lax.axis_size("gz"), lax.axis_size("gx"))
-    totals, halo = tv_exchange(pack_pair(0.0, change_part), art_volume, stages)
-    change_total = totals[0, 1]
-    padded = padded_from(art_volume, halo)
+    padded = padded_from(art_volume, halo_exchange(art_volume))
+    change_total = None
     smooth = art_volume
     for sweep_index in range(TV_STEPS):
         slope = tv_grad(pad_depth(padded))
         slope_part = jnp.sum(slope * slope)
-        totals, halo = tv_exchange(pack_pair(slope_part, 0.0), slope, stages)
+        totals, halo = tv_exchange(
+            pack_pair(slope_part, change_part if sweep_index == 0 else 0.0), slope, stages)
+        if sweep_index == 0:
+            change_total = totals[0, 1]
         slope_total = totals[0, 0]
         scale_now = step_gain * jnp.sqrt(change_total) / jnp.sqrt(slope_total + norm_floor)
         smooth = smooth - scale_now * slope

time: 279 us -> 270 us (0.968)
  Pallas kernels: 175 us -> 168 us
    pallas_call x5 -> x4, Pallas kernels: 82 us -> 62.5 us  [tv_exchange(): pl.pallas_call(functools.partial(tv_exchange_kernel, stages, (cells.shape...]
    pallas_call x0 -> x1, Pallas kernels: none -> 12.3 us  [halo_exchange(): pl.pallas_call(functools.partial(halo_exchange_kernel, (cells.shape[1], c...]
where the time goes in v2:
time: 270 us; the launch traced here: 265 us
  Pallas kernels  168 us (62%)
  other arithmetic  38.3 us (14%)
  local copies, waits for them, and re-layouts  30.9 us (11%)
  matrix products  19.4 us (7%)
  between operations  8.31 us (3%)
    pallas_call x4, Pallas kernels, tv_exchange(): pl.pallas_call(functools.partial(tv_exchange_kernel, stages, (cells.shape...  62.5 us
    pallas_call x2, Pallas kernels, vector_sum(): pl.pallas_call(functools.partial(vector_sum_kernel, n), out_shape=jax.Sha...  52.1 us
    pallas_call x4, Pallas kernels, block_apply(): pl.pallas_call(functools.partial(block_apply_kernel, group, transposed),...  41 us
    concatenate x5, local copies, waits for them, and re-layouts, faces_of(): jnp.concatenate([cells[-1], cells[0], cells[:, -1], cells[:, 0], cells[-1...  15.3 us
    pallas_call x1, Pallas kernels, halo_exchange(): pl.pallas_call(functools.partial(halo_exchange_kernel, (cells.shape[1], c...  12.3 us
    reduce_sum x4, other arithmetic, body(): slope_part = jnp.sum(slope * slope)  5.95 us
    dot_general x2, matrix products, body(): lax.dot_general(pick_voxel.astype(jnp.float32), product, (((0,), (0,)), (...  5.82 us
    mul x4, other arithmetic, tv_grad(): flow_z = diff_z * inverse  5.69 us

profile of v2, /device:TPU:1, one launch (start us, length us, event | category | flops | bytes accessed | tf_op | source)
XLA Modules:
  0.0 264.8 jit_solution(17993293804391688203)
XLA Ops:
  10.3 2.2 convert_reduce_fusion.1
  17.6 10.5 %shard_map.82 = f32[512,128]{1,0:T(8,128)} custom-call(bf16[512,128]{1,0:T(8,128)(2,1)} %fusion.8.x_ref, s32[512,1]{1,0:T(8,128)} %copy.36.blk_ref, bf16[64,128,128]{2,1,0:T(8,128)(2,1)} %w_ref.7), custom_call_target="tpu_custom_call" | custom-call | flops 1073741824 | bytes 2752512 | tf_op jit(solution)/shard_map/pallas_call | solution.py:289
  28.2 2.1 convolution_convert_fusion.3
  31.0 29.0 %shard_map.83 = bf16[32,16,256]{2,1,0:T(8,128)(2,1)} custom-call(bf16[32,16,256]{2,1,0:T(8,128)(2,1)} %pad_maximum_fusion.1.x_ref), custom_call_target="tpu_custom_call" | custom-call | tf_op jit(solution)/shard_map/pallas_call | solution.py:74
  65.2 10.1 %shard_map.84 = f32[512,128]{1,0:T(8,128)} custom-call(bf16[512,128]{1,0:T(8,128)(2,1)} %convolution_convert_fusion.2.x_ref, s32[512,1]{1,0:T(8,128)} %copy.36.blk_ref, bf16[64,128,128]{2,1,0:T(8,128)(2,1)} %w_ref.7), custom_call_target="tpu_custom_call" | custom-call | flops 1073741824 | bytes 2752512 | tf_op jit(solution)/shard_map/pallas_call | solution.py:289
  75.3 2.9 %fusion.6 = f32[1024,128]{1,0:T(8,128)S(1)} fusion(f32[1024,128]{1,0:T(8,128)S(1)} %convolution_add_fusion.1, s32[512]{0:T(512)S(1)} %bitcast.190, f32[512,128]{1,0:T(8,128)} %shard_map.84, pred[512]{0:T(512)(128)(4,1)S(1)} %iota_compare_fusion.27), kind=kOutput, calls=%fused_computation.26 | convolution fusion | flops 806027264 | bytes 1313280 | tf_op jit(solution)/shard_map/dot_general | solution.py:391
  80.4 10.1 %shard_map.85 = f32[512,128]{1,0:T(8,128)} custom-call(bf16[512,128]{1,0:T(8,128)(2,1)} %fusion.9.x_ref, s32[512,1]{1,0:T(8,128)} %copy.42.blk_ref, bf16[64,128,128]{2,1,0:T(8,128)(2,1)} %w_ref.7), custom_call_target="tpu_custom_call" | custom-call | flops 1073741824 | bytes 2752512 | tf_op jit(solution)/shard_map/pallas_call | solution.py:289
  90.5 2.1 convolution_convert_fusion.1
  93.3 23.1 %shard_map.86 = bf16[32,16,256]{2,1,0:T(8,128)(2,1)} custom-call(bf16[32,16,256]{2,1,0:T(8,128)(2,1)} %pad_maximum_fusion.2.x_ref), custom_call_target="tpu_custom_call" | custom-call | tf_op jit(solution)/shard_map/pallas_call | solution.py:74
  118.4 10.3 %shard_map.87 = f32[512,128]{1,0:T(8,128)} custom-call(bf16[512,128]{1,0:T(8,128)(2,1)} %convolution_convert_fusion.x_ref, s32[512,1]{1,0:T(8,128)} %copy.42.blk_ref, bf16[64,128,128]{2,1,0:T(8,128)(2,1)} %w_ref.7), custom_call_target="tpu_custom_call" | custom-call | flops 1073741824 | bytes 2752512 | tf_op jit(solution)/shard_map/pallas_call | solution.py:289
  128.7 2.9 %fusion.7 = f32[1024,128]{1,0:T(8,128)S(1)} fusion(f32[1024,128]{1,0:T(8,128)S(1)} %convolution_add_fusion, s32[512]{0:T(512)S(1)} %bitcast.186, f32[512,128]{1,0:T(8,128)} %shard_map.87, pred[512]{0:T(512)(128)(4,1)S(1)} %iota_compare_fusion.26), kind=kOutput, calls=%fused_computation.27 | convolution fusion | flops 806027264 | bytes 1313280 | tf_op jit(solution)/shard_map/dot_general | solution.py:391
  134.0 3.1 %concatenate.81.f_ref = f32[98,256]{1,0:T(8,128)} concatenate(f32[16,256]{1,0:T(8,128)S(1)} %bitcast.172, f32[16,256]{1,0:T(8,128)S(1)} %bitcast.167, f32[32,256]{1,0:T(8,128)S(1)} %get-tuple-element.74, f32[32,256]{1,0:T(8,128)S(1)} %get-tuple-element.73, f32[1,256]{1,0:T(1,128)S(1)} %get-tuple-element.72, f32[1,256]{1,0:T(1,128)S(1)} %get-tuple-element.71), dimensions={0} | concatenate | bytes 200704 | tf_op jit(solution)/shard_map/concatenate | solution.py:231
  137.1 12.3 %shard_map.88 = f32[98,256]{1,0:T(8,128)} custom-call(f32[98,256]{1,0:T(8,128)} %concatenate.81.f_ref), custom_call_target="tpu_custom_call" | custom-call | tf_op jit(solution)/shard_map/pallas_call | solution.py:216
  154.1 1.5 multiply_reduce_fusion.4
  156.9 3.1 %concatenate.86.f_ref = f32[98,256]{1,0:T(8,128)} concatenate(f32[16,256]{1,0:T(8,128)S(1)} %bitcast.173, f32[16,256]{1,0:T(8,128)S(1)} %bitcast.168, f32[32,256]{1,0:T(8,128)S(1)} %get-tuple-element.68, f32[32,256]{1,0:T(8,128)S(1)} %get-tuple-element.67, f32[1,256]{1,0:T(1,128)S(1)} %get-tuple-element.66, f32[1,256]{1,0:T(1,128)S(1)} %get-tuple-element.65), dimensions={0} | concatenate | bytes 200704 | tf_op jit(solution)/shard_map/concatenate | solution.py:231
  160.0 15.2 %shard_map.89 = (f32[8,128]{1,0:T(8,128)}, f32[98,256]{1,0:T(8,128)}) custom-call(f32[8,128]{1,0:T(8,128)} %broadcast_select_fusion.x_ref, f32[98,256]{1,0:T(8,128)} %concatenate.86.f_ref), custom_call_target="tpu_custom_call" | custom-call | tf_op jit(solution)/shard_map/pallas_call | solution.py:178
  182.9 1.5 multiply_reduce_fusion.2
  185.7 3.1 %concatenate.91.f_ref = f32[98,256]{1,0:T(8,128)} concatenate(f32[16,256]{1,0:T(8,128)S(1)} %bitcast.174, f32[16,256]{1,0:T(8,128)S(1)} %bitcast.169, f32[32,256]{1,0:T(8,128)S(1)} %get-tuple-element.62, f32[32,256]{1,0:T(8,128)S(1)} %get-tuple-element.61, f32[1,256]{1,0:T(1,128)S(1)} %get-tuple-element.60, f32[1,256]{1,0:T(1,128)S(1)} %get-tuple-element.59), dimensions={0} | concatenate | bytes 200704 | tf_op jit(solution)/shard_map/concatenate | solution.py:231
  188.8 15.7 %shard_map.90 = (f32[8,128]{1,0:T(8,128)}, f32[98,256]{1,0:T(8,128)}) custom-call(f32[8,128]{1,0:T(8,128)} %iota.59.x_ref, f32[98,256]{1,0:T(8,128)} %concatenate.91.f_ref), custom_call_target="tpu_custom_call" | custom-call | tf_op jit(solution)/shard_map/pallas_call | solution.py:178
  211.3 1.5 multiply_reduce_fusion.1
  214.1 3.1 %concatenate.96.f_ref = f32[98,256]{1,0:T(8,128)} concatenate(f32[16,256]{1,0:T(8,128)S(1)} %bitcast.175, f32[16,256]{1,0:T(8,128)S(1)} %bitcast.170, f32[32,256]{1,0:T(8,128)S(1)} %get-tuple-element.56, f32[32,256]{1,0:T(8,128)S(1)} %get-tuple-element.55, f32[1,256]{1,0:T(1,128)S(1)} %get-tuple-element.54, f32[1,256]{1,0:T(1,128)S(1)} %get-tuple-element.53), dimensions={0} | concatenate | bytes 200704 | tf_op jit(solution)/shard_map/concatenate | solution.py:231
  217.2 16.1 %shard_map.91 = (f32[8,128]{1,0:T(8,128)}, f32[98,256]{1,0:T(8,128)}) custom-call(f32[8,128]{1,0:T(8,128)} %iota.60.x_ref, f32[98,256]{1,0:T(8,128)} %concatenate.96.f_ref), custom_call_target="tpu_custom_call" | custom-call | tf_op jit(solution)/shard_map/pallas_call | solution.py:178
  242.8 3.1 %concatenate.101.f_ref = f32[98,256]{1,0:T(8,128)} concatenate(f32[16,256]{1,0:T(8,128)S(1)} %bitcast.176, f32[16,256]{1,0:T(8,128)S(1)} %bitcast.171, f32[32,256]{1,0:T(8,128)S(1)} %get-tuple-element.50, f32[32,256]{1,0:T(8,128)S(1)} %get-tuple-element.49, f32[1,256]{1,0:T(1,128)S(1)} %get-tuple-element.48, f32[1,256]{1,0:T(1,128)S(1)} %get-tuple-element.47), dimensions={0} | concatenate | bytes 200704 | tf_op jit(solution)/shard_map/concatenate | solution.py:231
  245.9 15.5 %shard_map.92 = (f32[8,128]{1,0:T(8,128)}, f32[98,256]{1,0:T(8,128)}) custom-call(f32[8,128]{1,0:T(8,128)} %iota.61.x_ref, f32[98,256]{1,0:T(8,128)} %concatenate.101.f_ref), custom_call_target="tpu_custom_call" | custom-call | tf_op jit(solution)/shard_map/pallas_call | solution.py:178
  (120 shorter events, 56.6 us)
Async XLA Ops:
  14.2 2.1 copy-start
  62.5 1.5 copy-start.1

commit v3 on v2

--- a/solution.py
+++ b/solution.py
@@ -111,6 +111,15 @@
     return position, total, peers
 
 
+def fill_faces(c_ref, faces, depth, width):
+    faces[pl.ds(0, depth)] = c_ref[width - 1]
+    faces[pl.ds(depth, depth)] = c_ref[0]
+    faces[pl.ds(2 * depth, width)] = c_ref[:, depth - 1, :]
+    faces[pl.ds(2 * depth + width, width)] = c_ref[:, 0, :]
+    faces[pl.ds(2 * depth + 2 * width, 1)] = c_ref[width - 1, pl.ds(0, 1), :]
+    faces[pl.ds(2 * depth + 2 * width + 1, 1)] = c_ref[0, pl.ds(depth - 1, 1), :]
+
+
 def halo_routes(depth, width):
     count_z, count_x = lax.axis_size("gz"), lax.axis_size("gx")
     z, x = lax.axis_index("gz"), lax.axis_index("gx")
@@ -126,8 +135,9 @@
     ]
 
 
-def tv_exchange_kernel(stages, shape, x_ref, f_ref, o_ref, h_ref, buf, recv, ssem, rsem, hrecv, hsend, hget):
+def tv_exchange_kernel(stages, shape, x_ref, c_ref, o_ref, h_ref, buf, recv, ssem, rsem, hrecv, hsend, hget, f_ref):
     routes = halo_routes(*shape)
+    fill_faces(c_ref, f_ref, *shape)
     plan = [_stage_peers(stage) for stage in stages]
     barrier = pltpu.get_barrier_semaphore()
     count = 0
@@ -173,11 +183,12 @@
 
 
 def tv_exchange(x, cells, stages):
-    faces = faces_of(cells)
+    width, depth, lanes = cells.shape
+    rows = 2 * depth + 2 * width + 2
     slots = sum(math.prod(size for _, _, size in stage) for stage in stages)
     return pl.pallas_call(
-        functools.partial(tv_exchange_kernel, stages, (cells.shape[1], cells.shape[0])),
-        out_shape=(jax.ShapeDtypeStruct(x.shape, x.dtype), jax.ShapeDtypeStruct(faces.shape, faces.dtype)),
+        functools.partial(tv_exchange_kernel, stages, (depth, width)),
+        out_shape=(jax.ShapeDtypeStruct(x.shape, x.dtype), jax.ShapeDtypeStruct((rows, lanes), cells.dtype)),
         in_specs=[pl.BlockSpec(memory_space=pltpu.VMEM)] * 2,
         out_specs=(pl.BlockSpec(memory_space=pltpu.VMEM), pl.BlockSpec(memory_space=pltpu.VMEM)),
         scratch_shapes=[
@@ -185,16 +196,18 @@
             pltpu.VMEM((slots,) + x.shape, x.dtype),
             pltpu.SemaphoreType.DMA((slots,)),
             pltpu.SemaphoreType.DMA((slots,)),
-            pltpu.VMEM(faces.shape, faces.dtype),
+            pltpu.VMEM((rows, lanes), cells.dtype),
             pltpu.SemaphoreType.DMA((6,)),
             pltpu.SemaphoreType.DMA((6,)),
+            pltpu.VMEM((rows, lanes), cells.dtype),
         ],
         compiler_params=pltpu.CompilerParams(collective_id=3, has_side_effects=True),
-    )(x, faces)
-
-
-def halo_exchange_kernel(shape, f_ref, h_ref, hrecv, hsend, hget):
+    )(x, cells)
+
+
+def halo_exchange_kernel(shape, c_ref, h_ref, hrecv, hsend, hget, f_ref):
     routes = halo_routes(*shape)
+    fill_faces(c_ref, f_ref, *shape)
     barrier = pltpu.get_barrier_semaphore()
     for _, _, target in routes:
         pl.semaphore_signal(barrier, inc=1, device_id=target, device_id_type=MESH)
@@ -212,19 +225,21 @@
 
 
 def halo_exchange(cells):
-    faces = faces_of(cells)
+    width, depth, lanes = cells.shape
+    rows = 2 * depth + 2 * width + 2
     return pl.pallas_call(
-        functools.partial(halo_exchange_kernel, (cells.shape[1], cells.shape[0])),
-        out_shape=jax.ShapeDtypeStruct(faces.shape, faces.dtype),
+        functools.partial(halo_exchange_kernel, (depth, width)),
+        out_shape=jax.ShapeDtypeStruct((rows, lanes), cells.dtype),
         in_specs=[pl.BlockSpec(memory_space=pltpu.VMEM)],
         out_specs=pl.BlockSpec(memory_space=pltpu.VMEM),
         scratch_shapes=[
-            pltpu.VMEM(faces.shape, faces.dtype),
+            pltpu.VMEM((rows, lanes), cells.dtype),
             pltpu.SemaphoreType.DMA((6,)),
             pltpu.SemaphoreType.DMA((6,)),
+            pltpu.VMEM((rows, lanes), cells.dtype),
         ],
         compiler_params=pltpu.CompilerParams(collective_id=4, has_side_effects=True),
-    )(faces)
+    )(cells)
 
 
 def faces_of(cells):

time: 270 us -> 262 us (0.970)
  local copies, waits for them, and re-layouts: 30.9 us -> 14.1 us
  other arithmetic: 38.3 us -> 44.4 us
  Pallas kernels: 168 us -> 171 us
    concatenate x13 -> x0, local copies, waits for them, and re-layouts: 15.5 us -> none  [the longest x5 15.3 us: faces_of(): jnp.concatenate([cells[-1], cells[0], cells[:, -1], cells[:, 0], cells[-1...]
    pallas_call x5, Pallas kernels: 74.8 us -> 78.1 us  [the longest x4 65.4 us: tv_exchange(): pl.pallas_call(functools.partial(tv_exchange_kernel, stages, (depth, widt...]
    reduce_sum x4, other arithmetic: 5.95 us -> 8.98 us  [body(): slope_part = jnp.sum(slope * slope)]
where the time goes in v3:
time: 262 us; the launch traced here: 257 us
  Pallas kernels  171 us (65%)
  other arithmetic  44.4 us (17%)
  matrix products  19.5 us (7%)
  local copies, waits for them, and re-layouts  14.1 us (5%)
  between operations  7.63 us (3%)
    pallas_call x4, Pallas kernels, tv_exchange(): pl.pallas_call(functools.partial(tv_exchange_kernel, stages, (depth, widt...  65.4 us
    pallas_call x2, Pallas kernels, vector_sum(): pl.pallas_call(functools.partial(vector_sum_kernel, n), out_shape=jax.Sha...  52.1 us
    pallas_call x4, Pallas kernels, block_apply(): pl.pallas_call(functools.partial(block_apply_kernel, group, transposed),...  41 us
    pallas_call x1, Pallas kernels, halo_exchange(): pl.pallas_call(functools.partial(halo_exchange_kernel, (depth, width)), o...  12.7 us
    reduce_sum x4, other arithmetic, body(): slope_part = jnp.sum(slope * slope)  8.98 us
    mul x4, other arithmetic, tv_grad(): flow_z = diff_z * inverse  6.58 us
    dot_general x2, matrix products, body(): lax.dot_general(pick_voxel.astype(jnp.float32), product, (((0,), (0,)), (...  5.84 us

profile of v3, /device:TPU:1, one launch (start us, length us, event | category | flops | bytes accessed | tf_op | source)
XLA Modules:
  0.0 256.8 jit_solution(4155172827331011736)
XLA Ops:
  9.9 2.2 convert_reduce_fusion.1
  17.3 10.6 %shard_map.82 = f32[512,128]{1,0:T(8,128)} custom-call(bf16[512,128]{1,0:T(8,128)(2,1)} %fusion.20.x_ref, s32[512,1]{1,0:T(8,128)} %copy.18.blk_ref, bf16[64,128,128]{2,1,0:T(8,128)(2,1)} %w_ref.7), custom_call_target="tpu_custom_call" | custom-call | flops 1073741824 | bytes 2752512 | tf_op jit(solution)/shard_map/pallas_call | solution.py:304
  27.8 2.1 convolution_convert_fusion.3
  30.7 29.0 %shard_map.83 = bf16[32,16,256]{2,1,0:T(8,128)(2,1)} custom-call(bf16[32,16,256]{2,1,0:T(8,128)(2,1)} %pad_maximum_fusion.8.x_ref), custom_call_target="tpu_custom_call" | custom-call | tf_op jit(solution)/shard_map/pallas_call | solution.py:74
  64.9 10.1 %shard_map.84 = f32[512,128]{1,0:T(8,128)} custom-call(bf16[512,128]{1,0:T(8,128)(2,1)} %convolution_convert_fusion.2.x_ref, s32[512,1]{1,0:T(8,128)} %copy.18.blk_ref, bf16[64,128,128]{2,1,0:T(8,128)(2,1)} %w_ref.7), custom_call_target="tpu_custom_call" | custom-call | flops 1073741824 | bytes 2752512 | tf_op jit(solution)/shard_map/pallas_call | solution.py:304
  75.0 2.9 %fusion.6 = f32[1024,128]{1,0:T(8,128)S(1)} fusion(f32[1024,128]{1,0:T(8,128)S(1)} %convolution_add_fusion.1, s32[512]{0:T(512)S(1)} %bitcast.102, f32[512,128]{1,0:T(8,128)} %shard_map.84, pred[512]{0:T(512)(128)(4,1)S(1)} %iota_compare_fusion.27), kind=kOutput, calls=%fused_computation.34 | convolution fusion | flops 806027264 | bytes 1313280 | tf_op jit(solution)/shard_map/dot_general | solution.py:406
  79.4 10.1 %shard_map.85 = f32[512,128]{1,0:T(8,128)} custom-call(bf16[512,128]{1,0:T(8,128)(2,1)} %fusion.21.x_ref, s32[512,1]{1,0:T(8,128)} %copy.21.blk_ref, bf16[64,128,128]{2,1,0:T(8,128)(2,1)} %w_ref.7), custom_call_target="tpu_custom_call" | custom-call | flops 1073741824 | bytes 2752512 | tf_op jit(solution)/shard_map/pallas_call | solution.py:304
  89.5 2.1 convolution_convert_fusion.1
  92.4 23.1 %shard_map.86 = bf16[32,16,256]{2,1,0:T(8,128)(2,1)} custom-call(bf16[32,16,256]{2,1,0:T(8,128)(2,1)} %pad_maximum_fusion.9.x_ref), custom_call_target="tpu_custom_call" | custom-call | tf_op jit(solution)/shard_map/pallas_call | solution.py:74
  117.5 10.3 %shard_map.87 = f32[512,128]{1,0:T(8,128)} custom-call(bf16[512,128]{1,0:T(8,128)(2,1)} %convolution_convert_fusion.x_ref, s32[512,1]{1,0:T(8,128)} %copy.21.blk_ref, bf16[64,128,128]{2,1,0:T(8,128)(2,1)} %w_ref.7), custom_call_target="tpu_custom_call" | custom-call | flops 1073741824 | bytes 2752512 | tf_op jit(solution)/shard_map/pallas_call | solution.py:304
  127.8 2.9 %fusion.7 = f32[1024,128]{1,0:T(8,128)S(1)} fusion(f32[1024,128]{1,0:T(8,128)S(1)} %convolution_add_fusion, s32[512]{0:T(512)S(1)} %bitcast.98, f32[512,128]{1,0:T(8,128)} %shard_map.87, pred[512]{0:T(512)(128)(4,1)S(1)} %iota_compare_fusion.26), kind=kOutput, calls=%fused_computation.35 | convolution fusion | flops 806027264 | bytes 1313280 | tf_op jit(solution)/shard_map/dot_general | solution.py:406
  133.1 12.7 %shard_map.88 = f32[98,256]{1,0:T(8,128)} custom-call(f32[32,16,256]{2,1,0:T(8,128)} %get-tuple-element.38.c_ref), custom_call_target="tpu_custom_call" | custom-call | tf_op jit(solution)/shard_map/pallas_call | solution.py:230
  151.0 2.2 multiply_reduce_fusion.4
  154.5 15.8 %shard_map.89 = (f32[8,128]{1,0:T(8,128)}, f32[98,256]{1,0:T(8,128)}) custom-call(f32[8,128]{1,0:T(8,128)} %broadcast_select_fusion.x_ref, f32[32,16,256]{2,1,0:T(8,128)} %get-tuple-element.34.c_ref), custom_call_target="tpu_custom_call" | custom-call | tf_op jit(solution)/shard_map/pallas_call | solution.py:189
  175.7 1.6 fusion.76
  178.4 2.2 multiply_reduce_fusion.2
  181.9 16.3 %shard_map.90 = (f32[8,128]{1,0:T(8,128)}, f32[98,256]{1,0:T(8,128)}) custom-call(f32[8,128]{1,0:T(8,128)} %iota.59.x_ref, f32[32,16,256]{2,1,0:T(8,128)} %get-tuple-element.30.c_ref), custom_call_target="tpu_custom_call" | custom-call | tf_op jit(solution)/shard_map/pallas_call | solution.py:189
  202.5 1.6 fusion.73
  205.2 2.2 multiply_reduce_fusion.1
  208.7 16.9 %shard_map.91 = (f32[8,128]{1,0:T(8,128)}, f32[98,256]{1,0:T(8,128)}) custom-call(f32[8,128]{1,0:T(8,128)} %iota.60.x_ref, f32[32,16,256]{2,1,0:T(8,128)} %get-tuple-element.26.c_ref), custom_call_target="tpu_custom_call" | custom-call | tf_op jit(solution)/shard_map/pallas_call | solution.py:189
  230.1 1.6 fusion.70
  232.8 2.2 multiply_reduce_fusion
  236.2 16.4 %shard_map.92 = (f32[8,128]{1,0:T(8,128)}, f32[98,256]{1,0:T(8,128)}) custom-call(f32[8,128]{1,0:T(8,128)} %iota.61.x_ref, f32[32,16,256]{2,1,0:T(8,128)} %get-tuple-element.22.c_ref), custom_call_target="tpu_custom_call" | custom-call | tf_op jit(solution)/shard_map/pallas_call | solution.py:189
  254.4 2.2 multiply_subtract_fusion
  (91 shorter events, 49.6 us)
Async XLA Ops:
  13.0 3.0 %copy-start.4 = (f32[32,16,256]{2,1,0:T(8,128)S(1)}, f32[32,16,256]{2,1,0:T(8,128)}, u32[]{:S(2)}) copy-start(f32[32,16,256]{2,1,0:T(8,128)} %param.8) | copy-start | bytes 1572868
  62.2 1.5 copy-start.5
  132.4 15.8 %copy-start = (f32[32,16,256]{2,1,0:T(8,128)S(1)}, f32[32,16,256]{2,1,0:T(8,128)}, u32[]{:S(2)}) copy-start(f32[32,16,256]{2,1,0:T(8,128)} %get-tuple-element.38.c_ref) | copy-start | bytes 1572868
  153.2 22.1 %copy-start.1 = (f32[32,16,256]{2,1,0:T(8,128)S(1)}, f32[32,16,256]{2,1,0:T(8,128)}, u32[]{:S(2)}) copy-start(f32[32,16,256]{2,1,0:T(8,128)} %get-tuple-element.34.c_ref) | copy-start | bytes 1572868
  180.6 21.7 %copy-start.2 = (f32[32,16,256]{2,1,0:T(8,128)S(1)}, f32[32,16,256]{2,1,0:T(8,128)}, u32[]{:S(2)}) copy-start(f32[32,16,256]{2,1,0:T(8,128)} %get-tuple-element.30.c_ref) | copy-start | bytes 1572868
  207.5 22.4 %copy-start.3 = (f32[32,16,256]{2,1,0:T(8,128)S(1)}, f32[32,16,256]{2,1,0:T(8,128)}, u32[]{:S(2)}) copy-start(f32[32,16,256]{2,1,0:T(8,128)} %get-tuple-element.26.c_ref) | copy-start | bytes 1572868

commit v4 on v3

--- a/solution.py
+++ b/solution.py
@@ -118,6 +118,23 @@
     faces[pl.ds(2 * depth + width, width)] = c_ref[:, 0, :]
     faces[pl.ds(2 * depth + 2 * width, 1)] = c_ref[width - 1, pl.ds(0, 1), :]
     faces[pl.ds(2 * depth + 2 * width + 1, 1)] = c_ref[0, pl.ds(depth - 1, 1), :]
+
+
+def write_halo(h_ref, hrecv, depth, width):
+    count_z, count_x = lax.axis_size("gz"), lax.axis_size("gx")
+    z, x = lax.axis_index("gz"), lax.axis_index("gx")
+    corner = 2 * depth + 2 * width
+    parts = [
+        (0, depth, z > 0),
+        (depth, depth, z < count_z - 1),
+        (2 * depth, width, x > 0),
+        (2 * depth + width, width, x < count_x - 1),
+        (corner, 1, (z > 0) & (x < count_x - 1)),
+        (corner + 1, 1, (z < count_z - 1) & (x > 0)),
+    ]
+    for row, rows, keep in parts:
+        values = hrecv[pl.ds(row, rows)]
+        h_ref[pl.ds(row, rows)] = jnp.where(keep, values, jnp.zeros_like(values))
 
 
 def halo_routes(depth, width):
@@ -179,7 +196,7 @@
     o_ref[...] = total
     for copy in halo:
         copy.wait()
-    h_ref[...] = hrecv[...]
+    write_halo(h_ref, hrecv, *shape)
 
 
 def tv_exchange(x, cells, stages):
@@ -221,7 +238,7 @@
         halo.append(copy)
     for copy in halo:
         copy.wait()
-    h_ref[...] = hrecv[...]
+    write_halo(h_ref, hrecv, *shape)
 
 
 def halo_exchange(cells):
@@ -248,16 +265,14 @@
 
 
 def padded_from(cells, halo):
-    count_z, count_x = lax.axis_size("gz"), lax.axis_size("gx")
-    z, x = lax.axis_index("gz"), lax.axis_index("gx")
     depth, width = cells.shape[1], cells.shape[0]
-    low_z = jnp.where(z > 0, halo[:depth], 0.0)[None]
-    high_z = jnp.where(z < count_z - 1, halo[depth:2 * depth], 0.0)[None]
-    low_x = jnp.where(x > 0, halo[2 * depth:2 * depth + width], 0.0)[:, None]
-    high_x = jnp.where(x < count_x - 1, halo[2 * depth + width:2 * depth + 2 * width], 0.0)[:, None]
+    low_z = halo[:depth][None]
+    high_z = halo[depth:2 * depth][None]
+    low_x = halo[2 * depth:2 * depth + width][:, None]
+    high_x = halo[2 * depth + width:2 * depth + 2 * width][:, None]
     corner = 2 * depth + 2 * width
-    low_z_high_x = jnp.where((z > 0) & (x < count_x - 1), halo[corner:corner + 1], 0.0)[None]
-    high_z_low_x = jnp.where((z < count_z - 1) & (x > 0), halo[corner + 1:corner + 2], 0.0)[None]
+    low_z_high_x = halo[corner:corner + 1][None]
+    high_z_low_x = halo[corner + 1:corner + 2][None]
     zero_line = jnp.zeros_like(cells[:1, :1])
     top = jnp.concatenate([zero_line, low_z, low_z_high_x], axis=1)
     middle = jnp.concatenate([low_x, cells, high_x], axis=1)

time: 262 us -> 262 us (level)
  other arithmetic: 44.4 us -> 35.2 us
  local copies, waits for them, and re-layouts: 14.1 us -> 23.2 us
    broadcast_in_dim x12 -> x0, other arithmetic: 9.2 us -> none  [the longest x4 3.12 us: padded_from(): low_x = jnp.where(x > 0, halo[2 * depth:2 * depth + width], 0.0)[:, None]]
    broadcast_in_dim x8 -> x16, local copies, waits for them, and re-layouts: 0.27 us -> 6.25 us  [the longest x4 3.11 us: padded_from(): low_z_high_x = halo[corner:corner + 1][None]]
    slice x0 -> x4, local copies, waits for them, and re-layouts: none -> 3.12 us  [padded_from(): low_x = halo[2 * depth:2 * depth + width][:, None]]
where the time goes in v4:
time: 262 us; the launch traced here: 257 us
  Pallas kernels  171 us (65%)
  other arithmetic  35.2 us (13%)
  local copies, waits for them, and re-layouts  23.2 us (9%)
  matrix products  19.5 us (7%)
  between operations  7.63 us (3%)
    pallas_call x4, Pallas kernels, tv_exchange(): pl.pallas_call(functools.partial(tv_exchange_kernel, stages, (depth, widt...  65.4 us
    pallas_call x2, Pallas kernels, vector_sum(): pl.pallas_call(functools.partial(vector_sum_kernel, n), out_shape=jax.Sha...  52.1 us
    pallas_call x4, Pallas kernels, block_apply(): pl.pallas_call(functools.partial(block_apply_kernel, group, transposed),...  41 us
    pallas_call x1, Pallas kernels, halo_exchange(): pl.pallas_call(functools.partial(halo_exchange_kernel, (depth, width)), o...  12.7 us
    reduce_sum x4, other arithmetic, body(): slope_part = jnp.sum(slope * slope)  8.98 us
    mul x4, other arithmetic, tv_grad(): flow_z = diff_z * inverse  6.58 us
    dot_general x2, matrix products, body(): lax.dot_general(pick_voxel.astype(jnp.float32), product, (((0,), (0,)), (...  5.84 us

profile of v4, /device:TPU:1, one launch (start us, length us, event | category | flops | bytes accessed | tf_op | source)
XLA Modules:
  0.0 256.7 jit_solution(7722617099772760169)
XLA Ops:
  9.9 2.2 convert_reduce_fusion.1
  17.3 10.6 %shard_map.82 = f32[512,128]{1,0:T(8,128)} custom-call(bf16[512,128]{1,0:T(8,128)(2,1)} %fusion.20.x_ref, s32[512,1]{1,0:T(8,128)} %copy.11.blk_ref, bf16[64,128,128]{2,1,0:T(8,128)(2,1)} %w_ref.7), custom_call_target="tpu_custom_call" | custom-call | flops 1073741824 | bytes 2752512 | tf_op jit(solution)/shard_map/pallas_call | solution.py:319
  27.8 2.1 convolution_convert_fusion.3
  30.7 29.0 %shard_map.83 = bf16[32,16,256]{2,1,0:T(8,128)(2,1)} custom-call(bf16[32,16,256]{2,1,0:T(8,128)(2,1)} %pad_maximum_fusion.8.x_ref), custom_call_target="tpu_custom_call" | custom-call | tf_op jit(solution)/shard_map/pallas_call | solution.py:74
  64.9 10.1 %shard_map.84 = f32[512,128]{1,0:T(8,128)} custom-call(bf16[512,128]{1,0:T(8,128)(2,1)} %convolution_convert_fusion.2.x_ref, s32[512,1]{1,0:T(8,128)} %copy.11.blk_ref, bf16[64,128,128]{2,1,0:T(8,128)(2,1)} %w_ref.7), custom_call_target="tpu_custom_call" | custom-call | flops 1073741824 | bytes 2752512 | tf_op jit(solution)/shard_map/pallas_call | solution.py:319
  75.0 2.9 %fusion.6 = f32[1024,128]{1,0:T(8,128)S(1)} fusion(f32[1024,128]{1,0:T(8,128)S(1)} %convolution_add_fusion.1, s32[512]{0:T(512)S(1)} %bitcast.88, f32[512,128]{1,0:T(8,128)} %shard_map.84, pred[512]{0:T(512)(128)(4,1)S(1)} %iota_compare_fusion.27), kind=kOutput, calls=%fused_computation.34 | convolution fusion | flops 806027264 | bytes 1313280 | tf_op jit(solution)/shard_map/dot_general | solution.py:421
  79.4 10.1 %shard_map.85 = f32[512,128]{1,0:T(8,128)} custom-call(bf16[512,128]{1,0:T(8,128)(2,1)} %fusion.21.x_ref, s32[512,1]{1,0:T(8,128)} %copy.14.blk_ref, bf16[64,128,128]{2,1,0:T(8,128)(2,1)} %w_ref.7), custom_call_target="tpu_custom_call" | custom-call | flops 1073741824 | bytes 2752512 | tf_op jit(solution)/shard_map/pallas_call | solution.py:319
  89.5 2.1 convolution_convert_fusion.1
  92.4 23.1 %shard_map.86 = bf16[32,16,256]{2,1,0:T(8,128)(2,1)} custom-call(bf16[32,16,256]{2,1,0:T(8,128)(2,1)} %pad_maximum_fusion.9.x_ref), custom_call_target="tpu_custom_call" | custom-call | tf_op jit(solution)/shard_map/pallas_call | solution.py:74
  117.5 10.3 %shard_map.87 = f32[512,128]{1,0:T(8,128)} custom-call(bf16[512,128]{1,0:T(8,128)(2,1)} %convolution_convert_fusion.x_ref, s32[512,1]{1,0:T(8,128)} %copy.14.blk_ref, bf16[64,128,128]{2,1,0:T(8,128)(2,1)} %w_ref.7), custom_call_target="tpu_custom_call" | custom-call | flops 1073741824 | bytes 2752512 | tf_op jit(solution)/shard_map/pallas_call | solution.py:319
  127.8 2.9 %fusion.7 = f32[1024,128]{1,0:T(8,128)S(1)} fusion(f32[1024,128]{1,0:T(8,128)S(1)} %convolution_add_fusion, s32[512]{0:T(512)S(1)} %bitcast.84, f32[512,128]{1,0:T(8,128)} %shard_map.87, pred[512]{0:T(512)(128)(4,1)S(1)} %iota_compare_fusion.26), kind=kOutput, calls=%fused_computation.35 | convolution fusion | flops 806027264 | bytes 1313280 | tf_op jit(solution)/shard_map/dot_general | solution.py:421
  133.1 12.7 %shard_map.88 = f32[98,256]{1,0:T(8,128)} custom-call(f32[32,16,256]{2,1,0:T(8,128)} %get-tuple-element.38.c_ref), custom_call_target="tpu_custom_call" | custom-call | tf_op jit(solution)/shard_map/pallas_call | solution.py:247
  151.0 2.2 multiply_reduce_fusion.4
  154.5 15.8 %shard_map.89 = (f32[8,128]{1,0:T(8,128)}, f32[98,256]{1,0:T(8,128)}) custom-call(f32[8,128]{1,0:T(8,128)} %broadcast_select_fusion.x_ref, f32[32,16,256]{2,1,0:T(8,128)} %get-tuple-element.34.c_ref), custom_call_target="tpu_custom_call" | custom-call | tf_op jit(solution)/shard_map/pallas_call | solution.py:206
  175.6 1.6 fusion.76
  178.3 2.2 multiply_reduce_fusion.2
  181.8 16.2 %shard_map.90 = (f32[8,128]{1,0:T(8,128)}, f32[98,256]{1,0:T(8,128)}) custom-call(f32[8,128]{1,0:T(8,128)} %iota.59.x_ref, f32[32,16,256]{2,1,0:T(8,128)} %get-tuple-element.30.c_ref), custom_call_target="tpu_custom_call" | custom-call | tf_op jit(solution)/shard_map/pallas_call | solution.py:206
  202.4 1.6 fusion.73
  205.1 2.2 multiply_reduce_fusion.1
  208.6 17.0 %shard_map.91 = (f32[8,128]{1,0:T(8,128)}, f32[98,256]{1,0:T(8,128)}) custom-call(f32[8,128]{1,0:T(8,128)} %iota.60.x_ref, f32[32,16,256]{2,1,0:T(8,128)} %get-tuple-element.26.c_ref), custom_call_target="tpu_custom_call" | custom-call | tf_op jit(solution)/shard_map/pallas_call | solution.py:206
  230.0 1.6 fusion.70
  232.6 2.2 multiply_reduce_fusion
  236.1 16.4 %shard_map.92 = (f32[8,128]{1,0:T(8,128)}, f32[98,256]{1,0:T(8,128)}) custom-call(f32[8,128]{1,0:T(8,128)} %iota.61.x_ref, f32[32,16,256]{2,1,0:T(8,128)} %get-tuple-element.22.c_ref), custom_call_target="tpu_custom_call" | custom-call | tf_op jit(solution)/shard_map/pallas_call | solution.py:206
  254.3 2.2 multiply_subtract_fusion
  (91 shorter events, 49.5 us)
Async XLA Ops:
  13.0 3.0 %copy-start.4 = (f32[32,16,256]{2,1,0:T(8,128)S(1)}, f32[32,16,256]{2,1,0:T(8,128)}, u32[]{:S(2)}) copy-start(f32[32,16,256]{2,1,0:T(8,128)} %param.8) | copy-start | bytes 1572868
  62.2 1.5 copy-start.5
  132.4 15.8 %copy-start = (f32[32,16,256]{2,1,0:T(8,128)S(1)}, f32[32,16,256]{2,1,0:T(8,128)}, u32[]{:S(2)}) copy-start(f32[32,16,256]{2,1,0:T(8,128)} %get-tuple-element.38.c_ref) | copy-start | bytes 1572868
  153.2 22.1 %copy-start.1 = (f32[32,16,256]{2,1,0:T(8,128)S(1)}, f32[32,16,256]{2,1,0:T(8,128)}, u32[]{:S(2)}) copy-start(f32[32,16,256]{2,1,0:T(8,128)} %get-tuple-element.34.c_ref) | copy-start | bytes 1572868
  180.6 21.7 %copy-start.2 = (f32[32,16,256]{2,1,0:T(8,128)S(1)}, f32[32,16,256]{2,1,0:T(8,128)}, u32[]{:S(2)}) copy-start(f32[32,16,256]{2,1,0:T(8,128)} %get-tuple-element.30.c_ref) | copy-start | bytes 1572868
  207.3 22.4 %copy-start.3 = (f32[32,16,256]{2,1,0:T(8,128)S(1)}, f32[32,16,256]{2,1,0:T(8,128)}, u32[]{:S(2)}) copy-start(f32[32,16,256]{2,1,0:T(8,128)} %get-tuple-element.26.c_ref) | copy-start | bytes 1572868

commit v5 on v4

--- a/solution.py
+++ b/solution.py
@@ -379,7 +379,7 @@
     row_weight = jnp.sum(weight_blocks, axis=2, dtype=jnp.float32)
     col_weight = jnp.sum(weight_blocks, axis=1, dtype=jnp.float32)
     n_blocks = weight_blocks.shape[0]
-    group = 4 if n_blocks % 4 == 0 else 1
+    group = 8 if n_blocks % 8 == 0 else 1
     current = volume
     for turn_index in range(view_order.shape[0]):
         view_index = view_order[turn_index]

time: 262 us -> 255 us (0.973)
  Pallas kernels: 171 us -> 165 us
    pallas_call x4, Pallas kernels: 41 us -> 34.6 us  [block_apply(): pl.pallas_call(functools.partial(block_apply_kernel, group, transposed),...]
where the time goes in v5:
time: 255 us; the launch traced here: 250 us
  Pallas kernels  165 us (65%)
  other arithmetic  35.2 us (14%)
  local copies, waits for them, and re-layouts  23.2 us (9%)
  matrix products  19.5 us (8%)
  between operations  7.63 us (3%)
    pallas_call x4, Pallas kernels, tv_exchange(): pl.pallas_call(functools.partial(tv_exchange_kernel, stages, (depth, widt...  65.3 us
    pallas_call x2, Pallas kernels, vector_sum(): pl.pallas_call(functools.partial(vector_sum_kernel, n), out_shape=jax.Sha...  52.1 us
    pallas_call x4, Pallas kernels, block_apply(): pl.pallas_call(functools.partial(block_apply_kernel, group, transposed),...  34.6 us
    pallas_call x1, Pallas kernels, halo_exchange(): pl.pallas_call(functools.partial(halo_exchange_kernel, (depth, width)), o...  12.7 us
    reduce_sum x4, other arithmetic, body(): slope_part = jnp.sum(slope * slope)  8.98 us
    mul x4, other arithmetic, tv_grad(): flow_z = diff_z * inverse  6.58 us
    dot_general x2, matrix products, body(): lax.dot_general(pick_voxel.astype(jnp.float32), product, (((0,), (0,)), (...  5.84 us

profile of v5, /device:TPU:1, one launch (start us, length us, event | category | flops | bytes accessed | tf_op | source)
XLA Modules:
  0.0 250.3 jit_solution(183423131732542487)
XLA Ops:
  9.9 2.2 convert_reduce_fusion.1
  17.3 9.0 %shard_map.82 = f32[512,128]{1,0:T(8,128)} custom-call(bf16[512,128]{1,0:T(8,128)(2,1)} %fusion.20.x_ref, s32[512,1]{1,0:T(8,128)} %copy.11.blk_ref, bf16[64,128,128]{2,1,0:T(8,128)(2,1)} %w_ref.7), custom_call_target="tpu_custom_call" | custom-call | flops 1073741824 | bytes 2752512 | tf_op jit(solution)/shard_map/pallas_call | solution.py:319
  26.2 2.1 convolution_convert_fusion.3
  29.1 29.0 %shard_map.83 = bf16[32,16,256]{2,1,0:T(8,128)(2,1)} custom-call(bf16[32,16,256]{2,1,0:T(8,128)(2,1)} %pad_maximum_fusion.8.x_ref), custom_call_target="tpu_custom_call" | custom-call | tf_op jit(solution)/shard_map/pallas_call | solution.py:74
  63.3 8.5 %shard_map.84 = f32[512,128]{1,0:T(8,128)} custom-call(bf16[512,128]{1,0:T(8,128)(2,1)} %convolution_convert_fusion.2.x_ref, s32[512,1]{1,0:T(8,128)} %copy.11.blk_ref, bf16[64,128,128]{2,1,0:T(8,128)(2,1)} %w_ref.7), custom_call_target="tpu_custom_call" | custom-call | flops 1073741824 | bytes 2752512 | tf_op jit(solution)/shard_map/pallas_call | solution.py:319
  71.8 2.9 %fusion.6 = f32[1024,128]{1,0:T(8,128)S(1)} fusion(f32[1024,128]{1,0:T(8,128)S(1)} %convolution_add_fusion.1, s32[512]{0:T(512)S(1)} %bitcast.88, f32[512,128]{1,0:T(8,128)} %shard_map.84, pred[512]{0:T(512)(128)(4,1)S(1)} %iota_compare_fusion.27), kind=kOutput, calls=%fused_computation.34 | convolution fusion | flops 806027264 | bytes 1313280 | tf_op jit(solution)/shard_map/dot_general | solution.py:421
  76.2 8.5 %shard_map.85 = f32[512,128]{1,0:T(8,128)} custom-call(bf16[512,128]{1,0:T(8,128)(2,1)} %fusion.21.x_ref, s32[512,1]{1,0:T(8,128)} %copy.14.blk_ref, bf16[64,128,128]{2,1,0:T(8,128)(2,1)} %w_ref.7), custom_call_target="tpu_custom_call" | custom-call | flops 1073741824 | bytes 2752512 | tf_op jit(solution)/shard_map/pallas_call | solution.py:319
  84.7 2.1 convolution_convert_fusion.1
  87.6 23.1 %shard_map.86 = bf16[32,16,256]{2,1,0:T(8,128)(2,1)} custom-call(bf16[32,16,256]{2,1,0:T(8,128)(2,1)} %pad_maximum_fusion.9.x_ref), custom_call_target="tpu_custom_call" | custom-call | tf_op jit(solution)/shard_map/pallas_call | solution.py:74
  112.7 8.7 %shard_map.87 = f32[512,128]{1,0:T(8,128)} custom-call(bf16[512,128]{1,0:T(8,128)(2,1)} %convolution_convert_fusion.x_ref, s32[512,1]{1,0:T(8,128)} %copy.14.blk_ref, bf16[64,128,128]{2,1,0:T(8,128)(2,1)} %w_ref.7), custom_call_target="tpu_custom_call" | custom-call | flops 1073741824 | bytes 2752512 | tf_op jit(solution)/shard_map/pallas_call | solution.py:319
  121.4 2.9 %fusion.7 = f32[1024,128]{1,0:T(8,128)S(1)} fusion(f32[1024,128]{1,0:T(8,128)S(1)} %convolution_add_fusion, s32[512]{0:T(512)S(1)} %bitcast.84, f32[512,128]{1,0:T(8,128)} %shard_map.87, pred[512]{0:T(512)(128)(4,1)S(1)} %iota_compare_fusion.26), kind=kOutput, calls=%fused_computation.35 | convolution fusion | flops 806027264 | bytes 1313280 | tf_op jit(solution)/shard_map/dot_general | solution.py:421
  126.7 12.7 %shard_map.88 = f32[98,256]{1,0:T(8,128)} custom-call(f32[32,16,256]{2,1,0:T(8,128)} %get-tuple-element.38.c_ref), custom_call_target="tpu_custom_call" | custom-call | tf_op jit(solution)/shard_map/pallas_call | solution.py:247
  141.9 1.6 fusion.79
  144.6 2.2 multiply_reduce_fusion.4
  148.1 15.8 %shard_map.89 = (f32[8,128]{1,0:T(8,128)}, f32[98,256]{1,0:T(8,128)}) custom-call(f32[8,128]{1,0:T(8,128)} %broadcast_select_fusion.x_ref, f32[32,16,256]{2,1,0:T(8,128)} %get-tuple-element.34.c_ref), custom_call_target="tpu_custom_call" | custom-call | tf_op jit(solution)/shard_map/pallas_call | solution.py:206
  169.3 1.6 fusion.76
  171.9 2.2 multiply_reduce_fusion.2
  175.5 16.3 %shard_map.90 = (f32[8,128]{1,0:T(8,128)}, f32[98,256]{1,0:T(8,128)}) custom-call(f32[8,128]{1,0:T(8,128)} %iota.59.x_ref, f32[32,16,256]{2,1,0:T(8,128)} %get-tuple-element.30.c_ref), custom_call_target="tpu_custom_call" | custom-call | tf_op jit(solution)/shard_map/pallas_call | solution.py:206
  196.1 1.6 fusion.73
  198.8 2.2 multiply_reduce_fusion.1
  202.3 16.9 %shard_map.91 = (f32[8,128]{1,0:T(8,128)}, f32[98,256]{1,0:T(8,128)}) custom-call(f32[8,128]{1,0:T(8,128)} %iota.60.x_ref, f32[32,16,256]{2,1,0:T(8,128)} %get-tuple-element.26.c_ref), custom_call_target="tpu_custom_call" | custom-call | tf_op jit(solution)/shard_map/pallas_call | solution.py:206
  226.3 2.2 multiply_reduce_fusion
  229.7 16.4 %shard_map.92 = (f32[8,128]{1,0:T(8,128)}, f32[98,256]{1,0:T(8,128)}) custom-call(f32[8,128]{1,0:T(8,128)} %iota.61.x_ref, f32[32,16,256]{2,1,0:T(8,128)} %get-tuple-element.22.c_ref), custom_call_target="tpu_custom_call" | custom-call | tf_op jit(solution)/shard_map/pallas_call | solution.py:206
  247.9 2.2 multiply_subtract_fusion
  (91 shorter events, 49.5 us)
Async XLA Ops:
  13.0 3.0 %copy-start.4 = (f32[32,16,256]{2,1,0:T(8,128)S(1)}, f32[32,16,256]{2,1,0:T(8,128)}, u32[]{:S(2)}) copy-start(f32[32,16,256]{2,1,0:T(8,128)} %param.8) | copy-start | bytes 1572868
  60.6 1.5 copy-start.5
  126.0 15.8 %copy-start = (f32[32,16,256]{2,1,0:T(8,128)S(1)}, f32[32,16,256]{2,1,0:T(8,128)}, u32[]{:S(2)}) copy-start(f32[32,16,256]{2,1,0:T(8,128)} %get-tuple-element.38.c_ref) | copy-start | bytes 1572868
  146.8 22.1 %copy-start.1 = (f32[32,16,256]{2,1,0:T(8,128)S(1)}, f32[32,16,256]{2,1,0:T(8,128)}, u32[]{:S(2)}) copy-start(f32[32,16,256]{2,1,0:T(8,128)} %get-tuple-element.34.c_ref) | copy-start | bytes 1572868
  174.2 21.7 %copy-start.2 = (f32[32,16,256]{2,1,0:T(8,128)S(1)}, f32[32,16,256]{2,1,0:T(8,128)}, u32[]{:S(2)}) copy-start(f32[32,16,256]{2,1,0:T(8,128)} %get-tuple-element.30.c_ref) | copy-start | bytes 1572868
  201.0 22.3 %copy-start.3 = (f32[32,16,256]{2,1,0:T(8,128)S(1)}, f32[32,16,256]{2,1,0:T(8,128)}, u32[]{:S(2)}) copy-start(f32[32,16,256]{2,1,0:T(8,128)} %get-tuple-element.26.c_ref) | copy-start | bytes 1572868

commit v6 on v5

--- a/solution.py
+++ b/solution.py
@@ -379,7 +379,7 @@
     row_weight = jnp.sum(weight_blocks, axis=2, dtype=jnp.float32)
     col_weight = jnp.sum(weight_blocks, axis=1, dtype=jnp.float32)
     n_blocks = weight_blocks.shape[0]
-    group = 8 if n_blocks % 8 == 0 else 1
+    group = 16 if n_blocks % 16 == 0 else 1
     current = volume
     for turn_index in range(view_order.shape[0]):
         view_index = view_order[turn_index]

time: 255 us -> 263 us (1.031)
  Pallas kernels: 165 us -> 172 us
    pallas_call x4, Pallas kernels: 34.6 us -> 42.1 us  [block_apply(): pl.pallas_call(functools.partial(block_apply_kernel, group, transposed),...]
where the time goes in v6:
time: 263 us; the launch traced here: 258 us
  Pallas kernels  172 us (65%)
  other arithmetic  35.2 us (13%)
  local copies, waits for them, and re-layouts  23.2 us (9%)
  matrix products  19.5 us (7%)
  between operations  7.63 us (3%)
    pallas_call x4, Pallas kernels, tv_exchange(): pl.pallas_call(functools.partial(tv_exchange_kernel, stages, (depth, widt...  65.2 us
    pallas_call x2, Pallas kernels, vector_sum(): pl.pallas_call(functools.partial(vector_sum_kernel, n), out_shape=jax.Sha...  52.1 us
    pallas_call x4, Pallas kernels, block_apply(): pl.pallas_call(functools.partial(block_apply_kernel, group, transposed),...  42.1 us
    pallas_call x1, Pallas kernels, halo_exchange(): pl.pallas_call(functools.partial(halo_exchange_kernel, (depth, width)), o...  12.6 us
    reduce_sum x4, other arithmetic, body(): slope_part = jnp.sum(slope * slope)  8.98 us
    mul x4, other arithmetic, tv_grad(): flow_z = diff_z * inverse  6.58 us
    dot_general x2, matrix products, body(): lax.dot_general(pick_voxel.astype(jnp.float32), product, (((0,), (0,)), (...  5.84 us

profile of v6, /device:TPU:1, one launch (start us, length us, event | category | flops | bytes accessed | tf_op | source)
XLA Modules:
  0.0 257.5 jit_solution(12544888059124205022)
XLA Ops:
  9.9 2.2 convert_reduce_fusion.1
  17.3 8.1 %shard_map.82 = f32[512,128]{1,0:T(8,128)} custom-call(bf16[512,128]{1,0:T(8,128)(2,1)} %fusion.20.x_ref, s32[512,1]{1,0:T(8,128)} %copy.11.blk_ref, bf16[64,128,128]{2,1,0:T(8,128)(2,1)} %w_ref.7), custom_call_target="tpu_custom_call" | custom-call | flops 1073741824 | bytes 2752512 | tf_op jit(solution)/shard_map/pallas_call | solution.py:319
  25.3 2.1 convolution_convert_fusion.3
  28.2 29.0 %shard_map.83 = bf16[32,16,256]{2,1,0:T(8,128)(2,1)} custom-call(bf16[32,16,256]{2,1,0:T(8,128)(2,1)} %pad_maximum_fusion.8.x_ref), custom_call_target="tpu_custom_call" | custom-call | tf_op jit(solution)/shard_map/pallas_call | solution.py:74
  62.4 7.7 %shard_map.84 = f32[512,128]{1,0:T(8,128)} custom-call(bf16[512,128]{1,0:T(8,128)(2,1)} %convolution_convert_fusion.2.x_ref, s32[512,1]{1,0:T(8,128)} %copy.11.blk_ref, bf16[64,128,128]{2,1,0:T(8,128)(2,1)} %w_ref.7), custom_call_target="tpu_custom_call" | custom-call | flops 1073741824 | bytes 2752512 | tf_op jit(solution)/shard_map/pallas_call | solution.py:319
  70.1 2.9 %fusion.6 = f32[1024,128]{1,0:T(8,128)S(1)} fusion(f32[1024,128]{1,0:T(8,128)S(1)} %convolution_add_fusion.1, s32[512]{0:T(512)S(1)} %bitcast.88, f32[512,128]{1,0:T(8,128)} %shard_map.84, pred[512]{0:T(512)(128)(4,1)S(1)} %iota_compare_fusion.27), kind=kOutput, calls=%fused_computation.34 | convolution fusion | flops 806027264 | bytes 1313280 | tf_op jit(solution)/shard_map/dot_general | solution.py:421
  74.5 18.7 %shard_map.85 = f32[512,128]{1,0:T(8,128)} custom-call(bf16[512,128]{1,0:T(8,128)(2,1)} %fusion.21.x_ref, s32[512,1]{1,0:T(8,128)} %copy.14.blk_ref, bf16[64,128,128]{2,1,0:T(8,128)(2,1)} %w_ref.7), custom_call_target="tpu_custom_call" | custom-call | flops 1073741824 | bytes 2752512 | tf_op jit(solution)/shard_map/pallas_call | solution.py:319
  93.2 2.1 convolution_convert_fusion.1
  96.0 23.1 %shard_map.86 = bf16[32,16,256]{2,1,0:T(8,128)(2,1)} custom-call(bf16[32,16,256]{2,1,0:T(8,128)(2,1)} %pad_maximum_fusion.9.x_ref), custom_call_target="tpu_custom_call" | custom-call | tf_op jit(solution)/shard_map/pallas_call | solution.py:74
  121.2 7.7 %shard_map.87 = f32[512,128]{1,0:T(8,128)} custom-call(bf16[512,128]{1,0:T(8,128)(2,1)} %convolution_convert_fusion.x_ref, s32[512,1]{1,0:T(8,128)} %copy.14.blk_ref, bf16[64,128,128]{2,1,0:T(8,128)(2,1)} %w_ref.7), custom_call_target="tpu_custom_call" | custom-call | flops 1073741824 | bytes 2752512 | tf_op jit(solution)/shard_map/pallas_call | solution.py:319
  128.9 2.9 %fusion.7 = f32[1024,128]{1,0:T(8,128)S(1)} fusion(f32[1024,128]{1,0:T(8,128)S(1)} %convolution_add_fusion, s32[512]{0:T(512)S(1)} %bitcast.84, f32[512,128]{1,0:T(8,128)} %shard_map.87, pred[512]{0:T(512)(128)(4,1)S(1)} %iota_compare_fusion.26), kind=kOutput, calls=%fused_computation.35 | convolution fusion | flops 806027264 | bytes 1313280 | tf_op jit(solution)/shard_map/dot_general | solution.py:421
  134.2 12.6 %shard_map.88 = f32[98,256]{1,0:T(8,128)} custom-call(f32[32,16,256]{2,1,0:T(8,128)} %get-tuple-element.38.c_ref), custom_call_target="tpu_custom_call" | custom-call | tf_op jit(solution)/shard_map/pallas_call | solution.py:247
  149.3 1.6 fusion.79
  152.0 2.2 multiply_reduce_fusion.4
  155.5 15.9 %shard_map.89 = (f32[8,128]{1,0:T(8,128)}, f32[98,256]{1,0:T(8,128)}) custom-call(f32[8,128]{1,0:T(8,128)} %broadcast_select_fusion.x_ref, f32[32,16,256]{2,1,0:T(8,128)} %get-tuple-element.34.c_ref), custom_call_target="tpu_custom_call" | custom-call | tf_op jit(solution)/shard_map/pallas_call | solution.py:206
  176.8 1.6 fusion.76
  179.5 2.2 multiply_reduce_fusion.2
  183.0 16.2 %shard_map.90 = (f32[8,128]{1,0:T(8,128)}, f32[98,256]{1,0:T(8,128)}) custom-call(f32[8,128]{1,0:T(8,128)} %iota.59.x_ref, f32[32,16,256]{2,1,0:T(8,128)} %get-tuple-element.30.c_ref), custom_call_target="tpu_custom_call" | custom-call | tf_op jit(solution)/shard_map/pallas_call | solution.py:206
  203.5 1.6 fusion.73
  206.2 2.2 multiply_reduce_fusion.1
  209.7 16.9 %shard_map.91 = (f32[8,128]{1,0:T(8,128)}, f32[98,256]{1,0:T(8,128)}) custom-call(f32[8,128]{1,0:T(8,128)} %iota.60.x_ref, f32[32,16,256]{2,1,0:T(8,128)} %get-tuple-element.26.c_ref), custom_call_target="tpu_custom_call" | custom-call | tf_op jit(solution)/shard_map/pallas_call | solution.py:206
  233.7 2.2 multiply_reduce_fusion
  237.2 16.2 %shard_map.92 = (f32[8,128]{1,0:T(8,128)}, f32[98,256]{1,0:T(8,128)}) custom-call(f32[8,128]{1,0:T(8,128)} %iota.61.x_ref, f32[32,16,256]{2,1,0:T(8,128)} %get-tuple-element.22.c_ref), custom_call_target="tpu_custom_call" | custom-call | tf_op jit(solution)/shard_map/pallas_call | solution.py:206
  255.2 2.2 multiply_subtract_fusion
  (91 shorter events, 49.5 us)
Async XLA Ops:
  13.0 3.0 %copy-start.4 = (f32[32,16,256]{2,1,0:T(8,128)S(1)}, f32[32,16,256]{2,1,0:T(8,128)}, u32[]{:S(2)}) copy-start(f32[32,16,256]{2,1,0:T(8,128)} %param.8) | copy-start | bytes 1572868
  59.7 1.5 copy-start.5
  133.5 15.7 %copy-start = (f32[32,16,256]{2,1,0:T(8,128)S(1)}, f32[32,16,256]{2,1,0:T(8,128)}, u32[]{:S(2)}) copy-start(f32[32,16,256]{2,1,0:T(8,128)} %get-tuple-element.38.c_ref) | copy-start | bytes 1572868
  154.2 22.2 %copy-start.1 = (f32[32,16,256]{2,1,0:T(8,128)S(1)}, f32[32,16,256]{2,1,0:T(8,128)}, u32[]{:S(2)}) copy-start(f32[32,16,256]{2,1,0:T(8,128)} %get-tuple-element.34.c_ref) | copy-start | bytes 1572868
  181.7 21.6 %copy-start.2 = (f32[32,16,256]{2,1,0:T(8,128)S(1)}, f32[32,16,256]{2,1,0:T(8,128)}, u32[]{:S(2)}) copy-start(f32[32,16,256]{2,1,0:T(8,128)} %get-tuple-element.30.c_ref) | copy-start | bytes 1572868
  208.5 22.4 %copy-start.3 = (f32[32,16,256]{2,1,0:T(8,128)S(1)}, f32[32,16,256]{2,1,0:T(8,128)}, u32[]{:S(2)}) copy-start(f32[32,16,256]{2,1,0:T(8,128)} %get-tuple-element.26.c_ref) | copy-start | bytes 1572868

commit v7 on v5

--- a/solution.py
+++ b/solution.py
@@ -29,8 +29,10 @@
 def vector_sum_kernel(n, x_ref, o_ref, recv, red, gath, ssem1, rsem1, ssem2, rsem2):
     me = lax.axis_index("gx")
     barrier = pltpu.get_barrier_semaphore()
-    for d in range(1, n):
+    @pl.loop(1, n)
+    def _(d):
         pl.semaphore_signal(barrier, inc=1, device_id=_peer("gx", lax.rem(me + d, n)), device_id_type=MESH)
+
     pl.semaphore_wait(barrier, n - 1)
 
     def scatter_copy(d):
@@ -152,16 +154,40 @@
     ]
 
 
+def _stage_info(stage):
+    index = {axis: lax.axis_index(axis) for axis, _, _ in stage}
+    digits = [lax.rem(index[axis] // stride, size) for axis, stride, size in stage]
+    total = 1
+    position = 0
+    for (_, _, size), digit in zip(stage, digits):
+        position = position * size + digit
+        total *= size
+
+    def peer(d):
+        q = lax.rem(position + d, total)
+        coords = dict(index)
+        rest = total
+        for (axis, stride, size), digit in zip(stage, digits):
+            rest //= size
+            coords[axis] = coords[axis] + (lax.rem(q // rest, size) - digit) * stride
+        return (coords.get("gz", lax.axis_index("gz")), coords.get("gx", lax.axis_index("gx")))
+
+    return position, total, peer
+
+
 def tv_exchange_kernel(stages, shape, x_ref, c_ref, o_ref, h_ref, buf, recv, ssem, rsem, hrecv, hsend, hget, f_ref):
     routes = halo_routes(*shape)
     fill_faces(c_ref, f_ref, *shape)
-    plan = [_stage_peers(stage) for stage in stages]
+    plan = [_stage_info(stage) for stage in stages]
     barrier = pltpu.get_barrier_semaphore()
     count = 0
-    for _, _, peers in plan:
-        for peer in peers:
-            pl.semaphore_signal(barrier, inc=1, device_id=peer, device_id_type=MESH)
-            count += 1
+    for _, size, peer in plan:
+
+        @pl.loop(1, size)
+        def _(d):
+            pl.semaphore_signal(barrier, inc=1, device_id=peer(d), device_id_type=MESH)
+
+        count += size - 1
     for _, _, target in routes:
         pl.semaphore_signal(barrier, inc=1, device_id=target, device_id_type=MESH)
         count += 1
@@ -173,23 +199,29 @@
             send_sem=hsend.at[k], recv_sem=hget.at[k], device_id=target, device_id_type=MESH)
         copy.start()
         halo.append(copy)
-    total = x_ref[...]
     slot = 0
-    for s, (position, size, peers) in enumerate(plan):
+    for s, (position, size, peer) in enumerate(plan):
         source = x_ref if s == 0 else buf.at[s - 1]
-        recv[slot] = total
-        sends = []
-        for d, peer in enumerate(peers, start=1):
-            copy = pltpu.make_async_remote_copy(
+        recv[slot] = x_ref[...] if s == 0 else buf[s - 1]
+
+        def sum_copy(d, source=source, slot=slot, peer=peer):
+            return pltpu.make_async_remote_copy(
                 src_ref=source, dst_ref=recv.at[slot + d], send_sem=ssem.at[slot + d],
-                recv_sem=rsem.at[slot + d], device_id=peer, device_id_type=MESH)
-            copy.start()
-            sends.append(copy)
-        for copy in sends:
-            copy.wait()
-        total = recv[slot + position]
-        for p in range(1, size):
-            total = total + recv[slot + lax.rem(position - p + size, size)]
+                recv_sem=rsem.at[slot + d], device_id=peer(d), device_id_type=MESH)
+
+        @pl.loop(1, size)
+        def _(d):
+            sum_copy(d).start()
+
+        @pl.loop(1, size)
+        def _(d):
+            sum_copy(d).wait()
+
+        total = lax.fori_loop(
+            1, size,
+            lambda p, acc, slot=slot, position=position, size=size:
+                acc + recv[slot + lax.rem(position - p + size, size)],
+            recv[slot + position])
         slot += size
         if s + 1 < len(plan):
             buf[s] = total

time: 255 us -> 258 us (1.012)
  Pallas kernels: 165 us -> 168 us
    pallas_call x4, Pallas kernels: 65.3 us -> 68 us  [tv_exchange(): pl.pallas_call(functools.partial(tv_exchange_kernel, stages, (depth, widt...]
where the time goes in v7:
time: 258 us; the launch traced here: 253 us
  Pallas kernels  168 us (65%)
  other arithmetic  35.2 us (14%)
  local copies, waits for them, and re-layouts  23.2 us (9%)
  matrix products  19.5 us (8%)
  between operations  7.63 us (3%)
    pallas_call x4, Pallas kernels, tv_exchange(): pl.pallas_call(functools.partial(tv_exchange_kernel, stages, (depth, widt...  68 us
    pallas_call x2, Pallas kernels, vector_sum(): pl.pallas_call(functools.partial(vector_sum_kernel, n), out_shape=jax.Sha...  52 us
    pallas_call x4, Pallas kernels, block_apply(): pl.pallas_call(functools.partial(block_apply_kernel, group, transposed),...  34.6 us
    pallas_call x1, Pallas kernels, halo_exchange(): pl.pallas_call(functools.partial(halo_exchange_kernel, (depth, width)), o...  13 us
    reduce_sum x4, other arithmetic, body(): slope_part = jnp.sum(slope * slope)  8.98 us
    mul x4, other arithmetic, tv_grad(): flow_z = diff_z * inverse  6.58 us
    dot_general x2, matrix products, body(): lax.dot_general(pick_voxel.astype(jnp.float32), product, (((0,), (0,)), (...  5.84 us

profile of v7, /device:TPU:1, one launch (start us, length us, event | category | flops | bytes accessed | tf_op | source)
XLA Modules:
  0.0 253.1 jit_solution(13391105667738646454)
XLA Ops:
  9.9 2.2 convert_reduce_fusion.1
  17.3 9.0 %shard_map.82 = f32[512,128]{1,0:T(8,128)} custom-call(bf16[512,128]{1,0:T(8,128)(2,1)} %fusion.20.x_ref, s32[512,1]{1,0:T(8,128)} %copy.11.blk_ref, bf16[64,128,128]{2,1,0:T(8,128)(2,1)} %w_ref.7), custom_call_target="tpu_custom_call" | custom-call | flops 1073741824 | bytes 2752512 | tf_op jit(solution)/shard_map/pallas_call | solution.py:351
  26.2 2.1 convolution_convert_fusion.3
  29.1 29.0 %shard_map.83 = bf16[32,16,256]{2,1,0:T(8,128)(2,1)} custom-call(bf16[32,16,256]{2,1,0:T(8,128)(2,1)} %pad_maximum_fusion.8.x_ref), custom_call_target="tpu_custom_call" | custom-call | tf_op jit(solution)/shard_map/pallas_call | solution.py:76
  63.3 8.5 %shard_map.84 = f32[512,128]{1,0:T(8,128)} custom-call(bf16[512,128]{1,0:T(8,128)(2,1)} %convolution_convert_fusion.2.x_ref, s32[512,1]{1,0:T(8,128)} %copy.11.blk_ref, bf16[64,128,128]{2,1,0:T(8,128)(2,1)} %w_ref.7), custom_call_target="tpu_custom_call" | custom-call | flops 1073741824 | bytes 2752512 | tf_op jit(solution)/shard_map/pallas_call | solution.py:351
  71.8 2.9 %fusion.6 = f32[1024,128]{1,0:T(8,128)S(1)} fusion(f32[1024,128]{1,0:T(8,128)S(1)} %convolution_add_fusion.1, s32[512]{0:T(512)S(1)} %bitcast.88, f32[512,128]{1,0:T(8,128)} %shard_map.84, pred[512]{0:T(512)(128)(4,1)S(1)} %iota_compare_fusion.27), kind=kOutput, calls=%fused_computation.34 | convolution fusion | flops 806027264 | bytes 1313280 | tf_op jit(solution)/shard_map/dot_general | solution.py:453
  76.3 8.5 %shard_map.85 = f32[512,128]{1,0:T(8,128)} custom-call(bf16[512,128]{1,0:T(8,128)(2,1)} %fusion.21.x_ref, s32[512,1]{1,0:T(8,128)} %copy.14.blk_ref, bf16[64,128,128]{2,1,0:T(8,128)(2,1)} %w_ref.7), custom_call_target="tpu_custom_call" | custom-call | flops 1073741824 | bytes 2752512 | tf_op jit(solution)/shard_map/pallas_call | solution.py:351
  84.8 2.1 convolution_convert_fusion.1
  87.6 23.0 %shard_map.86 = bf16[32,16,256]{2,1,0:T(8,128)(2,1)} custom-call(bf16[32,16,256]{2,1,0:T(8,128)(2,1)} %pad_maximum_fusion.9.x_ref), custom_call_target="tpu_custom_call" | custom-call | tf_op jit(solution)/shard_map/pallas_call | solution.py:76
  112.6 8.7 %shard_map.87 = f32[512,128]{1,0:T(8,128)} custom-call(bf16[512,128]{1,0:T(8,128)(2,1)} %convolution_convert_fusion.x_ref, s32[512,1]{1,0:T(8,128)} %copy.14.blk_ref, bf16[64,128,128]{2,1,0:T(8,128)(2,1)} %w_ref.7), custom_call_target="tpu_custom_call" | custom-call | flops 1073741824 | bytes 2752512 | tf_op jit(solution)/shard_map/pallas_call | solution.py:351
  121.3 2.9 %fusion.7 = f32[1024,128]{1,0:T(8,128)S(1)} fusion(f32[1024,128]{1,0:T(8,128)S(1)} %convolution_add_fusion, s32[512]{0:T(512)S(1)} %bitcast.84, f32[512,128]{1,0:T(8,128)} %shard_map.87, pred[512]{0:T(512)(128)(4,1)S(1)} %iota_compare_fusion.26), kind=kOutput, calls=%fused_computation.35 | convolution fusion | flops 806027264 | bytes 1313280 | tf_op jit(solution)/shard_map/dot_general | solution.py:453
  126.6 13.0 %shard_map.88 = f32[98,256]{1,0:T(8,128)} custom-call(f32[32,16,256]{2,1,0:T(8,128)} %get-tuple-element.38.c_ref), custom_call_target="tpu_custom_call" | custom-call | tf_op jit(solution)/shard_map/pallas_call | solution.py:279
  142.1 1.6 fusion.79
  144.8 2.2 multiply_reduce_fusion.4
  148.3 16.4 %shard_map.89 = (f32[8,128]{1,0:T(8,128)}, f32[98,256]{1,0:T(8,128)}) custom-call(f32[8,128]{1,0:T(8,128)} %broadcast_select_fusion.x_ref, f32[32,16,256]{2,1,0:T(8,128)} %get-tuple-element.34.c_ref), custom_call_target="tpu_custom_call" | custom-call | tf_op jit(solution)/shard_map/pallas_call | solution.py:238
  170.0 1.6 fusion.76
  172.7 2.2 multiply_reduce_fusion.2
  176.3 16.8 %shard_map.90 = (f32[8,128]{1,0:T(8,128)}, f32[98,256]{1,0:T(8,128)}) custom-call(f32[8,128]{1,0:T(8,128)} %iota.59.x_ref, f32[32,16,256]{2,1,0:T(8,128)} %get-tuple-element.30.c_ref), custom_call_target="tpu_custom_call" | custom-call | tf_op jit(solution)/shard_map/pallas_call | solution.py:238
  197.4 1.6 fusion.73
  200.1 2.2 multiply_reduce_fusion.1
  203.6 17.3 %shard_map.91 = (f32[8,128]{1,0:T(8,128)}, f32[98,256]{1,0:T(8,128)}) custom-call(f32[8,128]{1,0:T(8,128)} %iota.60.x_ref, f32[32,16,256]{2,1,0:T(8,128)} %get-tuple-element.26.c_ref), custom_call_target="tpu_custom_call" | custom-call | tf_op jit(solution)/shard_map/pallas_call | solution.py:238
  228.0 2.2 multiply_reduce_fusion
  231.4 17.5 %shard_map.92 = (f32[8,128]{1,0:T(8,128)}, f32[98,256]{1,0:T(8,128)}) custom-call(f32[8,128]{1,0:T(8,128)} %iota.61.x_ref, f32[32,16,256]{2,1,0:T(8,128)} %get-tuple-element.22.c_ref), custom_call_target="tpu_custom_call" | custom-call | tf_op jit(solution)/shard_map/pallas_call | solution.py:238
  250.7 2.2 multiply_subtract_fusion
  (91 shorter events, 49.5 us)
Async XLA Ops:
  13.0 3.0 %copy-start.4 = (f32[32,16,256]{2,1,0:T(8,128)S(1)}, f32[32,16,256]{2,1,0:T(8,128)}, u32[]{:S(2)}) copy-start(f32[32,16,256]{2,1,0:T(8,128)} %param.8) | copy-start | bytes 1572868
  60.6 1.5 copy-start.5
  125.9 16.1 %copy-start = (f32[32,16,256]{2,1,0:T(8,128)S(1)}, f32[32,16,256]{2,1,0:T(8,128)}, u32[]{:S(2)}) copy-start(f32[32,16,256]{2,1,0:T(8,128)} %get-tuple-element.38.c_ref) | copy-start | bytes 1572868
  147.0 22.7 %copy-start.1 = (f32[32,16,256]{2,1,0:T(8,128)S(1)}, f32[32,16,256]{2,1,0:T(8,128)}, u32[]{:S(2)}) copy-start(f32[32,16,256]{2,1,0:T(8,128)} %get-tuple-element.34.c_ref) | copy-start | bytes 1572868
  175.0 22.3 %copy-start.2 = (f32[32,16,256]{2,1,0:T(8,128)S(1)}, f32[32,16,256]{2,1,0:T(8,128)}, u32[]{:S(2)}) copy-start(f32[32,16,256]{2,1,0:T(8,128)} %get-tuple-element.30.c_ref) | copy-start | bytes 1572868
  202.4 22.7 %copy-start.3 = (f32[32,16,256]{2,1,0:T(8,128)S(1)}, f32[32,16,256]{2,1,0:T(8,128)}, u32[]{:S(2)}) copy-start(f32[32,16,256]{2,1,0:T(8,128)} %get-tuple-element.26.c_ref) | copy-start | bytes 1572868
